TPU v7x, 32 devices: a whole 2x2x4 slice. The times are simulated.
32 devices in a mesh: dp: 8 (over z, y), tensor: 4 (over x, core).
Axes of the slice: x: 2, y: 2, z: 4, core: 2. Of those that a mesh axis runs over, the one named last changes fastest.
Arguments:
- tokens: bfloat16 [2048, 1024], P('dp'), may hold values from -6 to 6
- norm_first: float32 [1024], replicated, may hold values from 0.25 to 1.75
- w_in: bfloat16 [1024, 3, 1024], P(None, None, 'tensor'), may hold values from -0.1875 to 0.1875
- conv_taps: float32 [3, 1024], P(None, 'tensor'), may hold values from -1 to 1
- w_out: bfloat16 [1024, 1024], P('tensor'), may hold values from -0.1875 to 0.1875
- norm_second: float32 [1024], replicated, may hold values from 0.25 to 1.75
- w_gate_up: bfloat16 [1024, 2, 4608], P(None, None, 'tensor'), may hold values from -0.1875 to 0.1875
- w_down: bfloat16 [4608, 1024], P('tensor'), may hold values from -0.09375 to 0.09375
- cotangent: bfloat16 [2048, 1024], P('dp'), may hold values from -6 to 6
Outputs:
- block_out: bfloat16 [2048, 1024], P('dp')
- grad_tokens: float32 [2048, 1024], P('dp')
- grad_norm_first: float32 [1024], replicated
- grad_w_in: float32 [1024, 3, 1024], P('dp', None, 'tensor')
- grad_taps: float32 [3, 1024], P(None, 'tensor')
- grad_w_out: float32 [1024, 1024], P('tensor', 'dp')
- grad_norm_second: float32 [1024], replicated
- grad_w_gate_up: float32 [1024, 2, 4608], P('dp', None, 'tensor')
- grad_w_down: float32 [4608, 1024], P('tensor', 'dp')
All inputs are finite; a program needn't handle non-finite values.
Results may differ from a plain program's by a relative error of at most 0.011.
Values sent between devices are 32-bit elements; how exact they have to be, the bound alone decides.
No kernel may reach another device: no remote copies, remote signals or barrier semaphores. Data moves between devices by JAX's collectives and lax.ppermute only.
A program may use at most 128 MiB of HBM per device.

v0:
```python
import functools

import jax
import jax.numpy as jnp
from jax import lax
from jax.experimental import pallas as pl
from jax.experimental.pallas import tpu as pltpu
from jax.sharding import PartitionSpec as P


eps = 1e-05


def shift_down(values, count):
    pad = jnp.zeros((count, values.shape[1]), values.dtype)
    return jnp.concatenate([pad, values[: values.shape[0] - count]], axis=0)


def shift_up(values, count):
    pad = jnp.zeros((count, values.shape[1]), values.dtype)
    return jnp.concatenate([values[count:], pad], axis=0)


def cross(left, right):
    return lax.dot_general(
        left, right, (((0,), (0,)), ((), ())), preferred_element_type=jnp.float32
    )


def by_transpose(left, right):
    return lax.dot_general(
        left, right, (((1,), (1,)), ((), ())), preferred_element_type=jnp.float32
    )


def body_scatter(tokens, norm_first, w_in, conv_taps, w_out, norm_second, w_gate_up, w_down, cotangent):
    rows, width = tokens.shape
    chans = w_in.shape[2]
    hid = w_down.shape[0]
    w_in_flat = w_in.reshape(width, 3 * chans)
    w_gu_flat = w_gate_up.reshape(width, 2 * hid)
    xf = tokens.astype(jnp.float32)
    s1 = lax.rsqrt(jnp.mean(xf * xf, axis=-1, keepdims=True) + eps)
    normed1 = (xf * s1 * norm_first).astype(jnp.bfloat16)
    proj = jnp.dot(normed1, w_in_flat, preferred_element_type=jnp.float32).reshape(rows, 3, chans)
    gate_b, gate_c, value = (proj[:, 0], proj[:, 1], proj[:, 2])
    mixed_in = gate_b * value
    conv = (
        conv_taps[0] * shift_down(mixed_in, 2)
        + conv_taps[1] * shift_down(mixed_in, 1)
        + conv_taps[2] * mixed_in
    )
    gated = (gate_c * conv).astype(jnp.bfloat16)
    mix = lax.psum(jnp.dot(gated, w_out, preferred_element_type=jnp.float32), "tensor")
    resid = xf + mix
    s2 = lax.rsqrt(jnp.mean(resid * resid, axis=-1, keepdims=True) + eps)
    normed2 = (resid * s2 * norm_second).astype(jnp.bfloat16)
    gate_up = jnp.dot(normed2, w_gu_flat, preferred_element_type=jnp.float32).reshape(rows, 2, hid)
    act, up = (gate_up[:, 0], gate_up[:, 1])
    sig = jax.nn.sigmoid(act)
    hidden = (act * sig * up).astype(jnp.bfloat16)
    ffn = lax.psum(jnp.dot(hidden, w_down, preferred_element_type=jnp.float32), "tensor")
    block_out = (resid + ffn).astype(jnp.bfloat16)
    cotf = cotangent.astype(jnp.float32)
    grad_down = cross(hidden, cotangent)
    d_hidden = by_transpose(cotangent, w_down)
    d_act = d_hidden * up * sig * (1.0 + act * (1.0 - sig))
    d_up = d_hidden * act * sig
    d_gu = jnp.stack([d_act, d_up], axis=1).astype(jnp.bfloat16).reshape(rows, 2 * hid)
    grad_gu = cross(normed2, d_gu).reshape(width, 2, hid)
    d_normed2 = lax.psum(by_transpose(d_gu, w_gu_flat), "tensor")
    gn2 = jnp.sum(d_normed2 * resid * s2, axis=0)
    weighted2 = d_normed2 * norm_second
    d_resid = (
        cotf + s2 * weighted2 - resid * s2**3 * jnp.mean(weighted2 * resid, axis=-1, keepdims=True)
    )
    d_resid_b = d_resid.astype(jnp.bfloat16)
    grad_out = cross(gated, d_resid_b)
    d_gated = by_transpose(d_resid_b, w_out)
    d_c = d_gated * conv
    d_conv = d_gated * gate_c
    gtaps = jnp.stack(
        [
            jnp.sum(d_conv * shift_down(mixed_in, 2), axis=0),
            jnp.sum(d_conv * shift_down(mixed_in, 1), axis=0),
            jnp.sum(d_conv * mixed_in, axis=0),
        ],
        axis=0,
    )
    d_mixed = (
        conv_taps[2] * d_conv
        + conv_taps[1] * shift_up(d_conv, 1)
        + conv_taps[0] * shift_up(d_conv, 2)
    )
    d_proj = (
        jnp.stack([d_mixed * value, d_c, d_mixed * gate_b], axis=1)
        .astype(jnp.bfloat16)
        .reshape(rows, 3 * chans)
    )
    grad_in = cross(normed1, d_proj).reshape(width, 3, chans)
    d_normed1 = lax.psum(by_transpose(d_proj, w_in_flat), "tensor")
    gn1 = jnp.sum(d_normed1 * xf * s1, axis=0)
    weighted1 = d_normed1 * norm_first
    grad_tokens = (
        d_resid + s1 * weighted1 - xf * s1**3 * jnp.mean(weighted1 * xf, axis=-1, keepdims=True)
    )
    shared_in, shared_out, shared_gu, shared_down = (
        lax.psum_scatter(grad_in, "dp", scatter_dimension=0, tiled=True),
        lax.psum_scatter(grad_out, "dp", scatter_dimension=1, tiled=True),
        lax.psum_scatter(grad_gu, "dp", scatter_dimension=0, tiled=True),
        lax.psum_scatter(grad_down, "dp", scatter_dimension=1, tiled=True),
    )
    sum_taps, sum_n1, sum_n2 = lax.psum((gtaps, gn1, gn2), "dp")
    return (
        block_out,
        grad_tokens,
        sum_n1,
        shared_in,
        sum_taps,
        shared_out,
        sum_n2,
        shared_gu,
        shared_down,
    )


def gathers(dp, tensor, rows, width, hid):
    powers = all(size > 1 and size & (size - 1) == 0 for size in (dp, tensor))
    whole = rows % (8 * tensor) == 0 and hid % (128 * tensor) == 0
    return powers and whole and width % (128 * dp) == 0 and dp * rows <= 2 * width


def far_kernel(
    where,
    *refs,
    rows,
    share,
    block,
):
    pieces, refs = refs[:8], refs[8:]
    norm, x_near, c_near, h_near, dg_near, du_near, wg, wu, wd = refs[:9]
    gu_own, gu_there, down_own, down_there, x_all, c_all, xs, cs, dg, du, hidden = refs[9:]
    f32, bf16 = jnp.float32, jnp.bfloat16

    @pl.when(pl.program_id(0) == 0)
    def _():
        x_all[:rows] = x_near[...]
        c_all[:rows] = c_near[...]
        for i in range(4):
            at = pl.ds(rows + i * share, share)
            x_all[at] = (pieces[i][...] * norm[...]).astype(bf16)
            c_all[at] = pieces[4 + i][...].astype(bf16)
        for i in range(2):
            at = pl.ds(pl.multiple_of(where[i] * block, block), block)
            xs[:, i * block : (i + 1) * block] = x_all[:, at]
            cs[:, i * block : (i + 1) * block] = c_all[:, at]

    act = jnp.dot(x_all[rows:], wg[...], preferred_element_type=f32)
    up = jnp.dot(x_all[rows:], wu[...], preferred_element_type=f32)
    d_hidden = by_transpose(c_all[rows:], wd[...])
    sig = jax.nn.sigmoid(act)
    hidden[:rows] = h_near[...]
    dg[:rows] = dg_near[...]
    du[:rows] = du_near[...]
    hidden[rows:] = (act * sig * up).astype(bf16)
    dg[rows:] = (d_hidden * up * sig * (1.0 + act * (1.0 - sig))).astype(bf16)
    du[rows:] = (d_hidden * act * sig).astype(bf16)
    for i, grad in enumerate((dg, du)):
        both = cross(xs[...], grad[...])
        gu_own[i] = both[:block]
        gu_there[i] = both[block:]
    both = cross(hidden[...], cs[...])
    down_own[...] = both[:, :block]
    down_there[...] = both[:, block:]


def far_grads(where, pieces, norm, x_near, c_near, h_near, d_gu_near, w_gu, w_down):
    rows, width = x_near.shape
    hid = w_down.shape[0]
    share = pieces[0].shape[0]
    block = 128
    tokens = rows + 4 * share
    step = max(size for size in range(128, 513, 128) if hid % size == 0)
    steps = hid // step
    f32, bf16 = jnp.float32, jnp.bfloat16

    def whole(array):
        return pl.BlockSpec(
            array.shape, lambda j, _: (0,) * array.ndim, pipeline_mode=pl.Buffered(1)
        )

    return pl.pallas_call(
        functools.partial(far_kernel, rows=rows, share=share, block=block),
        out_shape=(
            *[jax.ShapeDtypeStruct((2, block, hid), f32)] * 2,
            *[jax.ShapeDtypeStruct((hid, block), f32)] * 2,
        ),
        grid_spec=pltpu.PrefetchScalarGridSpec(
            num_scalar_prefetch=1,
            grid=(steps,),
            in_specs=[
                *[whole(piece) for piece in pieces],
                whole(norm),
                whole(x_near),
                whole(c_near),
                pl.BlockSpec((rows, step), lambda j, _: (0, j)),
                pl.BlockSpec((rows, step), lambda j, _: (0, j)),
                pl.BlockSpec((rows, step), lambda j, _: (0, j + steps)),
                pl.BlockSpec((width, step), lambda j, _: (0, j)),
                pl.BlockSpec((width, step), lambda j, _: (0, j + steps)),
                pl.BlockSpec((step, width), lambda j, _: (j, 0)),
            ],
            out_specs=[
                *[pl.BlockSpec((2, block, step), lambda j, _: (0, 0, j))] * 2,
                *[pl.BlockSpec((step, block), lambda j, _: (j, 0))] * 2,
            ],
            scratch_shapes=[
                *[pltpu.VMEM((tokens, width), bf16)] * 2,
                *[pltpu.VMEM((tokens, 2 * block), bf16)] * 2,
                *[pltpu.VMEM((tokens, step), bf16)] * 3,
            ],
        ),
        compiler_params=pltpu.CompilerParams(vmem_limit_bytes=48 << 20),
        cost_estimate=pl.CostEstimate(
            flops=2 * hid * (3 * 4 * share * width + 3 * tokens * 2 * block),
            bytes_accessed=8 * share * width * 4 + 6 * hid * width + 24 * hid * block,
            transcendentals=4 * share * hid,
        ),
        name="far_grads",
    )(where, *pieces, norm, x_near, c_near, h_near, d_gu_near, d_gu_near, w_gu, w_gu, w_down)


def body_gather(
    dp,
    tensor,
    tokens,
    norm_first,
    w_in,
    conv_taps,
    w_out,
    norm_second,
    w_gate_up,
    w_down,
    cotangent,
):
    rows, width = tokens.shape
    chans = w_in.shape[2]
    hid = w_down.shape[0]
    half = rows // 2
    line = dp // 2
    block = width // dp
    chips = tensor // 2
    share = half // chips
    f32, bf16 = jnp.float32, jnp.bfloat16
    w_in_flat = w_in.reshape(width, 3 * chans)
    core = lax.axis_index("tensor") % 2
    place = lax.axis_index("dp")
    along, side = place // 2, place % 2
    is_second = core.astype(f32)
    is_first = 1.0 - is_second

    def to_core(values):
        return lax.ppermute(values, "tensor", [(i, i ^ 1) for i in range(tensor)])

    def to_side(values):
        return lax.ppermute(values, "dp", [(i, i ^ 1) for i in range(dp)])

    def to_line(values, count):
        return lax.ppermute(values, "dp", [(i, (i + 2 * count) % dp) for i in range(dp)])

    def over_chips(values):
        stride = 2
        while stride < tensor:
            there = lax.ppermute(values, "tensor", [(i, i ^ stride) for i in range(tensor)])
            stride *= 2
            if stride < tensor:
                values = values + there
        return values, there

    def mine(values):
        return lax.dynamic_slice_in_dim(values, core * half, half, 0)

    def other(values):
        return lax.dynamic_slice_in_dim(values, (1 - core) * half, half, 0)

    def ordered(own, partner):
        return jnp.concatenate(
            [own * is_first + partner * is_second, own * is_second + partner * is_first], axis=0
        )

    def after(values, *others):
        return lax.optimization_barrier((values, *others))[0]

    def summed(first, second, product):
        sent = product(second)
        own = product(after(first, sent))
        return over_chips(own + to_core(sent))

    chip = lax.axis_index("tensor") // 2

    def spread(quarter):
        return [to_line(quarter, k) for k in range(1, line)]

    def gathered(pieces):
        near = jnp.concatenate(pieces, axis=0)
        stride = 2
        while stride < tensor:
            there = lax.ppermute(near, "tensor", [(i, i ^ stride) for i in range(tensor)])
            stride *= 2
            if stride < tensor:
                near = jnp.concatenate([near, there], axis=0)
        return near, there, to_core(near), to_core(there)

    def conv_forward(tok):
        s1 = lax.rsqrt(jnp.mean(tok * tok, axis=-1, keepdims=True) + eps)
        normed1 = (tok * s1 * norm_first).astype(bf16)
        proj = jnp.dot(normed1, w_in_flat, preferred_element_type=f32)
        gate_b, gate_c, value = (
            proj[:, :chans],
            proj[:, chans : 2 * chans],
            proj[:, 2 * chans :],
        )
        mixed_in = gate_b * value
        conv = (
            conv_taps[0] * shift_down(mixed_in, 2)
            + conv_taps[1] * shift_down(mixed_in, 1)
            + conv_taps[2] * mixed_in
        )
        gated = (gate_c * conv).astype(bf16)
        return s1, normed1, gate_b, gate_c, value, mixed_in, conv, gated

    def conv_backward(d_resid_b, saved):
        _, _, gate_b, gate_c, value, mixed_in, conv, _ = saved
        d_gated = by_transpose(d_resid_b, w_out)
        d_c = d_gated * conv
        d_conv = d_gated * gate_c
        gtaps = jnp.stack(
            [
                jnp.sum(d_conv * shift_down(mixed_in, 2), axis=0),
                jnp.sum(d_conv * shift_down(mixed_in, 1), axis=0),
                jnp.sum(d_conv * mixed_in, axis=0),
            ],
            axis=0,
        )
        d_mixed = (
            conv_taps[2] * d_conv
            + conv_taps[1] * shift_up(d_conv, 1)
            + conv_taps[0] * shift_up(d_conv, 2)
        )
        d_proj = jnp.concatenate([d_mixed * value, d_c, d_mixed * gate_b], axis=1).astype(bf16)
        return d_proj, gtaps

    def ffn(normed2, cot):
        gate_up = jnp.dot(normed2, w_gu_flat, preferred_element_type=f32)
        act, up = gate_up[:, :hid], gate_up[:, hid:]
        sig = jax.nn.sigmoid(act)
        hidden = (act * sig * up).astype(bf16)
        d_hidden = by_transpose(cot, w_down)
        d_act = d_hidden * up * sig * (1.0 + act * (1.0 - sig))
        d_up = d_hidden * act * sig
        return hidden, jnp.concatenate([d_act, d_up], axis=1).astype(bf16)

    xf = tokens.astype(f32)
    saved = conv_forward(xf)
    s1, normed1, gated = saved[0], saved[1], saved[7]
    mix, mix_there = summed(
        mine(gated), other(gated), lambda part: jnp.dot(part, w_out, preferred_element_type=f32)
    )

    cot_quarter = lax.dynamic_slice_in_dim(cotangent, core * half + chip * share, share, 0)
    cot_pieces = spread(cot_quarter.astype(f32))
    w_gu_flat = after(w_gate_up, gated).reshape(width, 2 * hid)
    mix_there, w_gu_flat = lax.optimization_barrier((mix_there, w_gu_flat))
    beside = to_side(after(tokens, gated).astype(f32))

    resid = mine(xf) + (mix + mix_there)
    s2 = lax.rsqrt(jnp.mean(resid * resid, axis=-1, keepdims=True) + eps)
    scaled = resid * s2
    scaled_there = to_core(scaled)
    normed2_pieces = spread(lax.dynamic_slice_in_dim(scaled, chip * share, share, 0))
    cot_far = gathered([after(p, scaled) for p in cot_pieces])
    normed2_near = (jnp.concatenate([scaled, scaled_there], axis=0) * norm_second).astype(
        bf16
    )
    cot_near = jnp.concatenate([mine(cotangent), other(cotangent)], axis=0)
    hidden_near, d_gu_near = ffn(normed2_near, cot_near)
    d_normed2_chip, d_normed2_there = summed(
        d_gu_near[:half], d_gu_near[half:], lambda part: by_transpose(part, w_gu_flat)
    )

    saved_beside = conv_forward(after(beside, d_gu_near))

    d_normed2 = d_normed2_chip + d_normed2_there
    gn2 = jnp.sum(d_normed2 * resid * s2, axis=0)
    weighted2 = d_normed2 * norm_second
    d_resid = (
        mine(cotangent).astype(f32)
        + s2 * weighted2
        - resid * s2**3 * jnp.mean(weighted2 * resid, axis=-1, keepdims=True)
    )
    d_resid_seq = ordered(d_resid, to_core(d_resid)).astype(bf16)
    d_resid_beside = to_side(d_resid)

    d_proj, gtaps = conv_backward(d_resid_seq, saved)
    d_normed1, d_normed1_there = summed(
        mine(d_proj), other(d_proj), lambda part: by_transpose(part, w_in_flat)
    )

    d_resid_beside = after(d_resid_beside, d_proj)
    d_resid_next = ordered(d_resid_beside, to_core(d_resid_beside)).astype(bf16)
    d_proj_beside, _ = conv_backward(d_resid_next, saved_beside)
    both = [
        jnp.concatenate(pair, axis=0)
        for pair in (
            (normed1, saved_beside[1]),
            (d_resid_seq, d_resid_next),
            (d_proj, d_proj_beside),
            (gated, saved_beside[7]),
        )
    ]

    def columns(values, start):
        return lax.dynamic_slice_in_dim(values, start, block, 1)

    def conv_part(k):
        start = (lax.rem(along + k, line) * 2 + side) * block
        grads = jnp.concatenate(
            [cross(columns(both[0], start), both[2]), cross(columns(both[1], start), both[3])],
            axis=1,
        )
        return grads

    parts = [to_line(conv_part(k), k) for k in range(1, line)]
    kept = conv_part(0)
    total = sum(parts, kept)
    grad_in = total[:, : 3 * chans].reshape(block, 3, chans)
    grad_out = total[:, 3 * chans :].T

    normed2_far = gathered([after(p, d_normed2_chip) for p in normed2_pieces])
    gu_here, gu_there, down_here, down_there = far_grads(
        jnp.stack([place, along * 2 + 1 - side]),
        (*normed2_far, *cot_far),
        norm_second.reshape(1, width),
        normed2_near,
        cot_near,
        hidden_near,
        d_gu_near,
        w_gu_flat,
        w_down,
    )
    down_there = to_side(down_there)
    gu_there = to_side(gu_there)
    grad_down = down_here + down_there
    grad_gu = (gu_here + gu_there).swapaxes(0, 1)

    d_normed1 = d_normed1 + d_normed1_there
    xf_mine, s1_mine = mine(xf), mine(s1)
    weighted1 = d_normed1 * norm_first
    grad_mine = (
        d_resid
        + s1_mine * weighted1
        - xf_mine * s1_mine**3 * jnp.mean(weighted1 * xf_mine, axis=-1, keepdims=True)
    )
    grad_tokens = ordered(grad_mine, to_core(grad_mine))

    hidden_late = after(hidden_near, d_proj)
    out, out_there = summed(
        hidden_late[:half],
        hidden_late[half:],
        lambda part: jnp.dot(part, w_down, preferred_element_type=f32),
    )
    out_mine = resid + (out + out_there)
    block_out = ordered(out_mine, to_core(out_mine)).astype(bf16)

    gn1 = jnp.sum(d_normed1 * xf_mine * s1_mine, axis=0)
    gains = jnp.concatenate([gn1, gn2])
    gains = gains + to_core(gains)
    small = jnp.concatenate([gains, gtaps.reshape(-1)])
    small = small + to_side(small)
    stride = 2
    while stride < dp:
        there = lax.ppermute(small, "dp", [(i, i ^ stride) for i in range(dp)])
        small = small + there
        stride *= 2
    return (
        block_out,
        grad_tokens,
        small[:width],
        grad_in,
        small[2 * width : 2 * width + gtaps.size].reshape(gtaps.shape),
        grad_out,
        small[width : 2 * width],
        grad_gu,
        grad_down,
    )


def solution(mesh):
    dp, tensor = mesh.shape["dp"], mesh.shape["tensor"]

    def body(*args):
        if gathers(dp, tensor, *args[0].shape, args[7].shape[0] * tensor):
            return body_gather(dp, tensor, *args)
        return body_scatter(*args)

    return jax.shard_map(
        body,
        mesh=mesh,
        in_specs=(
            P("dp", None),
            P(),
            P(None, None, "tensor"),
            P(None, "tensor"),
            P("tensor", None),
            P(),
            P(None, None, "tensor"),
            P("tensor", None),
            P("dp", None),
        ),
        out_specs=(
            P("dp", None),
            P("dp", None),
            P(),
            P("dp", None, "tensor"),
            P(None, "tensor"),
            P("tensor", "dp"),
            P(),
            P("dp", None, "tensor"),
            P("tensor", "dp"),
        ),
        check_vma=False,
    )
```

profile of v0, /device:TPU:0, one launch (start us, length us, event | category | flops | bytes accessed | tf_op | source)
XLA Modules:
  0.0 220.5 jit_solution(17615099240925314353)
XLA Ops:
  0.7 1.3 multiply_reduce_fusion.1
  2.0 1.8 copy.23
  5.9 2.0 multiply_convert_fusion.12
  8.8 1.5 collective-permute-done
  10.5 2.9 %collective-permute-start.1 = (f32[128,1024]{1,0:T(8,128)S(1)}, f32[128,1024]{1,0:T(8,128)}, u32[]{:S(2)}, u32[]{:S(2)}) collective-permute-start(f32[128,1024]{1,0:T(8,128)S(1)} %convolution_add_fusion.3), channel_id=1, source_target_pairs={{0,2},{1,3},{2,0},{3,1},{4,6},{5,7},{6,4},{7,5},{8,10},{9,11},{10,... | collective-permute-start | bytes 1572872 | tf_op jit(solution)/shard_map/ppermute | solution.py:274
  13.5 1.6 dynamic-slice_convert_fusion
  15.1 1.6 collective-permute-start.28
  16.7 2.6 %collective-permute-start.29 = (f32[64,1024]{1,0:T(8,128)}, f32[64,1024]{1,0:T(8,128)}, u32[]{:S(2)}, u32[]{:S(2)}) collective-permute-start(f32[64,1024]{1,0:T(8,128)} %dynamic-slice_convert_fusion), channel_id=1, source_target_pairs={{0,16},{4,20},{8,24},{12,28},{16,0},{20,4},{24,8},{28,12},{1,17},{... | collective-permute-start | bytes 786440 | tf_op jit(solution)/shard_map/ppermute | solution.py:269
  19.3 1.3 collective-permute-start.30
  21.8 1.5 collective-permute-start.16
  23.4 5.7 %copy.31 = bf16[128,8,2,1152]{3,1,2,0:T(8,128)(2,1)} copy(bf16[128,8,2,1152]{3,2,1,0:T(2,128)(2,1)} %bitcast.66) | data formatting | bytes 9437184
  30.0 1.3 multiply_reduce_fusion.6
  32.2 4.2 %collective-permute-start.22 = (f32[64,1024]{1,0:T(8,128)S(1)}, f32[64,1024]{1,0:T(8,128)S(1)}, u32[]{:S(2)}, u32[]{:S(2)}) collective-permute-start(f32[64,1024]{1,0:T(8,128)S(1)} %constant_dynamic-slice_fusion), channel_id=1, source_target_pairs={{0,8},{4,12},{8,16},{12,20},{16,24},{20,28},{24,0},{28,4},{1,9},{5... | collective-permute-start | bytes 786440 | tf_op jit(solution)/shard_map/ppermute | solution.py:269
  36.7 1.7 collective-permute-start.23
  38.5 14.9 %collective-permute-start.24 = (f32[64,1024]{1,0:T(8,128)S(1)}, f32[64,1024]{1,0:T(8,128)S(1)}, u32[]{:S(2)}, u32[]{:S(2)}) collective-permute-start(f32[64,1024]{1,0:T(8,128)S(1)} %constant_dynamic-slice_fusion), channel_id=1, source_target_pairs={{0,24},{4,28},{8,0},{12,4},{16,8},{20,12},{24,16},{28,20},{1,25},{... | collective-permute-start | bytes 786440 | tf_op jit(solution)/shard_map/ppermute | solution.py:269
  53.4 1.7 constant_dynamic-update-slice_fusion.5
  55.1 1.7 constant_dynamic-update-slice_fusion.4
  56.7 1.7 constant_dynamic-update-slice_fusion.3.refs_4_
  58.6 3.9 %fusion.65 = f32[256,2304]{1,0:T(8,128)S(1)} fusion(bf16[256,1024]{1,0:T(8,128)(2,1)S(1)} %fusion.refs_9_, bf16[1024,2304]{1,0:T(8,128)(2,1)} %bitcast.51), kind=kOutput, calls=%fused_computation.159 | convolution fusion | flops 1207959552 | bytes 7602176 | tf_op jit(solution)/shard_map/dot_general | solution.py:354
  62.5 1.4 multiply_convert_fusion
  63.9 1.6 fusion.3
  67.3 1.4 multiply_reduce_fusion
  68.6 1.6 convolution_add_fusion.2
  70.3 1.6 collective-permute-start.4
  72.7 25.9 %collective-permute-done.4 = f32[128,1024]{1,0:T(8,128)S(1)} collective-permute-done((f32[128,1024]{1,0:T(8,128)S(1)}, f32[128,1024]{1,0:T(8,128)S(1)}, u32[]{:S(2)}, u32[]{:S(2)}) %collective-permute-start.4) | collective-permute-done | bytes 524320 | tf_op jit(solution)/shard_map/ppermute | solution.py:274
  99.1 1.7 multiply_convert_fusion.3
  100.9 1.5 fusion.66
  102.9 12.2 %collective-permute-done.25.refs_1_ = f32[192,1024]{1,0:T(8,128)} collective-permute-done((f32[192,1024]{1,0:T(8,128)S(1)}, f32[192,1024]{1,0:T(8,128)}, u32[]{:S(2)}, u32[]{:S(2)}) %collective-permute-start.25) | collective-permute-done | bytes 786464 | tf_op jit(solution)/shard_map/ppermute | solution.py:308
  115.1 1.5 collective-permute-start.17
  117.9 10.7 %collective-permute-done.17 = f32[128,1024]{1,0:T(8,128)} collective-permute-done((f32[128,1024]{1,0:T(8,128)S(1)}, f32[128,1024]{1,0:T(8,128)}, u32[]{:S(2)}, u32[]{:S(2)}) %collective-permute-start.17) | collective-permute-done | bytes 524320 | tf_op jit(solution)/shard_map/ppermute | solution.py:266
  128.6 1.3 fusion.15
  131.4 1.2 fusion.17
  133.2 1.3 add_convert_fusion.1
  142.2 1.6 collective-permute-start.10
  143.8 2.1 collective-permute-start.20
  145.8 2.0 collective-permute-start.19
  147.8 16.5 %far_grads.1 = (f32[2,128,1152]{2,1,0:T(8,128)}, f32[2,128,1152]{2,1,0:T(8,128)}, f32[1152,128]{1,0:T(8,128)S(1)}, f32[1152,128]{1,0:T(8,128)}) custom-call(s32[2]{0:T(128)S(1)} %pad_add_fusion.where, f32[192,1024]{1,0:T(8,128)S(1)} %constant_dynamic-update-slice_fusion.refs_0_, f32[192,1024]{1,0:T(8,128)} %collective-permute-done.25.refs_1_, ...), custom_call_target="tpu_custom_call" | custom-call | flops 7247757312 | bytes 16908288 | tf_op jit(solution)/shard_map/far_grads/pallas_call | solution.py:192
  164.4 2.1 collective-permute-done.10
  167.9 1.5 collective-permute-start.34
  170.1 26.3 %collective-permute-done.13 = f32[2816]{0:T(1024)S(1)} collective-permute-done((f32[2816]{0:T(1024)S(1)}, f32[2816]{0:T(1024)S(1)}, u32[]{:S(2)}, u32[]{:S(2)}) %collective-permute-start.13) | collective-permute-done | bytes 11296 | tf_op jit(solution)/shard_map/ppermute | solution.py:266
  196.4 1.5 collective-permute-start.35
  198.8 3.0 %collective-permute-done.14 = f32[2816]{0:T(1024)S(1)} collective-permute-done((f32[2816]{0:T(1024)S(1)}, f32[2816]{0:T(1024)S(1)}, u32[]{:S(2)}, u32[]{:S(2)}) %collective-permute-start.14) | collective-permute-done | bytes 11296 | tf_op jit(solution)/shard_map/ppermute | solution.py:482
  201.8 2.0 collective-permute-start.15
  207.8 3.5 %collective-permute-done.35 = f32[1152,128]{1,0:T(8,128)S(1)} collective-permute-done((f32[1152,128]{1,0:T(8,128)}, f32[1152,128]{1,0:T(8,128)S(1)}, u32[]{:S(2)}, u32[]{:S(2)}) %collective-permute-start.35) | collective-permute-done | bytes 589856 | tf_op jit(solution)/shard_map/ppermute | solution.py:266
  212.2 1.2 add_convert_fusion.3
  214.2 1.2 multiply_add_fusion.1
  217.1 1.4 add_bitcast_fusion
  218.5 1.9 copy.29
  (230 shorter events, 30.9 us)
Async XLA Ops:
  8.0 12.7 %copy-start.18 = (bf16[256,1024]{1,0:T(8,128)(2,1)S(1)}, bf16[256,1024]{1,0:T(8,128)(2,1)}, u32[]{:S(2)}) copy-start(bf16[256,1024]{1,0:T(8,128)(2,1)} %param.9) | copy-start | bytes 1572868
  8.2 2.1 collective-permute-start
  10.5 18.8 %collective-permute-start.1 = (f32[128,1024]{1,0:T(8,128)S(1)}, f32[128,1024]{1,0:T(8,128)}, u32[]{:S(2)}, u32[]{:S(2)}) collective-permute-start(f32[128,1024]{1,0:T(8,128)S(1)} %convolution_add_fusion.3), channel_id=1, source_target_pairs={{0,2},{1,3},{2,0},{3,1},{4,6},{5,7},{6,4},{7,5},{8,10},{9,11},{10,... | collective-permute-start | bytes 1572872 | tf_op jit(solution)/shard_map/ppermute | solution.py:274
  15.1 17.1 %collective-permute-start.28 = (f32[64,1024]{1,0:T(8,128)}, f32[64,1024]{1,0:T(8,128)}, u32[]{:S(2)}, u32[]{:S(2)}) collective-permute-start(f32[64,1024]{1,0:T(8,128)} %dynamic-slice_convert_fusion), channel_id=1, source_target_pairs={{0,8},{4,12},{8,16},{12,20},{16,24},{20,28},{24,0},{28,4},{1,9},{5... | collective-permute-start | bytes 786440 | tf_op jit(solution)/shard_map/ppermute | solution.py:269
  16.7 20.0 %collective-permute-start.29 = (f32[64,1024]{1,0:T(8,128)}, f32[64,1024]{1,0:T(8,128)}, u32[]{:S(2)}, u32[]{:S(2)}) collective-permute-start(f32[64,1024]{1,0:T(8,128)} %dynamic-slice_convert_fusion), channel_id=1, source_target_pairs={{0,16},{4,20},{8,24},{12,28},{16,0},{20,4},{24,8},{28,12},{1,17},{... | collective-permute-start | bytes 786440 | tf_op jit(solution)/shard_map/ppermute | solution.py:269
  19.3 19.2 %collective-permute-start.30 = (f32[64,1024]{1,0:T(8,128)}, f32[64,1024]{1,0:T(8,128)}, u32[]{:S(2)}, u32[]{:S(2)}) collective-permute-start(f32[64,1024]{1,0:T(8,128)} %dynamic-slice_convert_fusion), channel_id=1, source_target_pairs={{0,24},{4,28},{8,0},{12,4},{16,8},{20,12},{24,16},{28,20},{1,25},{... | collective-permute-start | bytes 786440 | tf_op jit(solution)/shard_map/ppermute | solution.py:269
  21.8 45.0 %collective-permute-start.16 = (f32[256,1024]{1,0:T(8,128)}, f32[256,1024]{1,0:T(8,128)}, u32[]{:S(2)}, u32[]{:S(2)}) collective-permute-start(f32[256,1024]{1,0:T(8,128)} %convert_element_type.46), channel_id=1, source_target_pairs={{0,4},{4,0},{8,12},{12,8},{16,20},{20,16},{24,28},{28,24},{1,5},{5... | collective-permute-start | bytes 3145736 | tf_op jit(solution)/shard_map/ppermute | solution.py:266
  29.3 33.1 %copy-start.26 = (bf16[128,1024]{1,0:T(8,128)(2,1)}, bf16[128,1024]{1,0:T(8,128)(2,1)S(1)}, u32[]{:S(2)}) copy-start(bf16[128,1024]{1,0:T(8,128)(2,1)S(1)} %get-tuple-element.104) | copy-start | bytes 786436
  31.3 27.1 %copy-start.2 = (f32[1024]{0:T(1024)S(1)}, f32[1024]{0:T(1024)}, u32[]{:S(2)}) copy-start(f32[1024]{0:T(1024)} %param.14) | copy-start | bytes 12292
  31.4 27.0 %collective-permute-start.2 = (f32[128,1024]{1,0:T(8,128)S(1)}, f32[128,1024]{1,0:T(8,128)S(1)}, u32[]{:S(2)}, u32[]{:S(2)}) collective-permute-start(f32[128,1024]{1,0:T(8,128)S(1)} %broadcast_multiply_fusion), channel_id=1, source_target_pairs={{0,1},{1,0},{2,3},{3,2},{4,5},{5,4},{6,7},{7,6},{8,9},{9,8},{10,11... | collective-permute-start | bytes 1572872 | tf_op jit(solution)/shard_map/ppermute | solution.py:263
  32.2 39.7 %collective-permute-start.22 = (f32[64,1024]{1,0:T(8,128)S(1)}, f32[64,1024]{1,0:T(8,128)S(1)}, u32[]{:S(2)}, u32[]{:S(2)}) collective-permute-start(f32[64,1024]{1,0:T(8,128)S(1)} %constant_dynamic-slice_fusion), channel_id=1, source_target_pairs={{0,8},{4,12},{8,16},{12,20},{16,24},{20,28},{24,0},{28,4},{1,9},{5... | collective-permute-start | bytes 786440 | tf_op jit(solution)/shard_map/ppermute | solution.py:269
  36.7 35.2 %collective-permute-start.23 = (f32[64,1024]{1,0:T(8,128)S(1)}, f32[64,1024]{1,0:T(8,128)S(1)}, u32[]{:S(2)}, u32[]{:S(2)}) collective-permute-start(f32[64,1024]{1,0:T(8,128)S(1)} %constant_dynamic-slice_fusion), channel_id=1, source_target_pairs={{0,16},{4,20},{8,24},{12,28},{16,0},{20,4},{24,8},{28,12},{1,17},{... | collective-permute-start | bytes 786440 | tf_op jit(solution)/shard_map/ppermute | solution.py:269
  38.5 33.5 %collective-permute-start.24 = (f32[64,1024]{1,0:T(8,128)S(1)}, f32[64,1024]{1,0:T(8,128)S(1)}, u32[]{:S(2)}, u32[]{:S(2)}) collective-permute-start(f32[64,1024]{1,0:T(8,128)S(1)} %constant_dynamic-slice_fusion), channel_id=1, source_target_pairs={{0,24},{4,28},{8,0},{12,4},{16,8},{20,12},{24,16},{28,20},{1,25},{... | collective-permute-start | bytes 786440 | tf_op jit(solution)/shard_map/ppermute | solution.py:269
  65.5 3.1 %collective-permute-start.3 = (f32[128,1024]{1,0:T(8,128)S(1)}, f32[128,1024]{1,0:T(8,128)S(1)}, u32[]{:S(2)}, u32[]{:S(2)}) collective-permute-start(f32[128,1024]{1,0:T(8,128)S(1)} %fusion.3), channel_id=1, source_target_pairs={{0,1},{1,0},{2,3},{3,2},{4,5},{5,4},{6,7},{7,6},{8,9},{9,8},{10,11... | collective-permute-start | bytes 1572872 | tf_op jit(solution)/shard_map/ppermute | solution.py:263
  66.7 35.7 %collective-permute-start.31 = (f32[192,1024]{1,0:T(8,128)}, f32[192,1024]{1,0:T(8,128)}, u32[]{:S(2)}, u32[]{:S(2)}) collective-permute-start(f32[192,1024]{1,0:T(8,128)} %constant_dynamic-update-slice_fusion.3.refs_4_), channel_id=1, source_target_pairs={{0,2},{1,3},{2,0},{3,1},{4,6},{5,7},{6,4},{7,5},{8,10},{9,11},{10,... | collective-permute-start | bytes 2359304 | tf_op jit(solution)/shard_map/ppermute | solution.py:308
  70.3 28.3 %copy-start.9 = (f32[128,1024]{1,0:T(8,128)S(1)}, f32[128,1024]{1,0:T(8,128)}, u32[]{:S(2)}) copy-start(f32[128,1024]{1,0:T(8,128)} %copy-done.8) | copy-start | bytes 1572868
  70.3 28.3 %collective-permute-start.4 = (f32[128,1024]{1,0:T(8,128)S(1)}, f32[128,1024]{1,0:T(8,128)S(1)}, u32[]{:S(2)}, u32[]{:S(2)}) collective-permute-start(f32[128,1024]{1,0:T(8,128)S(1)} %convolution_add_fusion.2), channel_id=1, source_target_pairs={{0,2},{1,3},{2,0},{3,1},{4,6},{5,7},{6,4},{7,5},{8,10},{9,11},{10,... | collective-permute-start | bytes 1572872 | tf_op jit(solution)/shard_map/ppermute | solution.py:274
  71.9 26.9 %copy-start.27 = (bf16[128,1024]{1,0:T(8,128)(2,1)S(1)}, bf16[128,1024]{1,0:T(8,128)(2,1)}, u32[]{:S(2)}) copy-start(bf16[128,1024]{1,0:T(8,128)(2,1)} %copy-done.26) | copy-start | bytes 786436
  71.9 70.3 %collective-permute-start.32 = (f32[192,1024]{1,0:T(8,128)}, f32[192,1024]{1,0:T(8,128)}, u32[]{:S(2)}, u32[]{:S(2)}) collective-permute-start(f32[192,1024]{1,0:T(8,128)} %constant_dynamic-update-slice_fusion.3.refs_4_), channel_id=1, source_target_pairs={{0,1},{1,0},{2,3},{3,2},{4,5},{5,4},{6,7},{7,6},{8,9},{9,8},{10,11... | collective-permute-start | bytes 2359304 | tf_op jit(solution)/shard_map/ppermute | solution.py:263
  72.1 43.0 %collective-permute-start.25 = (f32[192,1024]{1,0:T(8,128)S(1)}, f32[192,1024]{1,0:T(8,128)}, u32[]{:S(2)}, u32[]{:S(2)}) collective-permute-start(f32[192,1024]{1,0:T(8,128)S(1)} %constant_dynamic-update-slice_fusion.refs_0_), channel_id=1, source_target_pairs={{0,2},{1,3},{2,0},{3,1},{4,6},{5,7},{6,4},{7,5},{8,10},{9,11},{10,... | collective-permute-start | bytes 2359304 | tf_op jit(solution)/shard_map/ppermute | solution.py:308
  99.0 17.6 %copy-start.24 = (f32[128,1024]{1,0:T(8,128)}, f32[128,1024]{1,0:T(8,128)S(1)}, u32[]{:S(2)}) copy-start(f32[128,1024]{1,0:T(8,128)S(1)} %multiply_subtract_fusion.1) | copy-start | bytes 1572868
  99.0 17.6 %collective-permute-start.5 = (f32[128,1024]{1,0:T(8,128)S(1)}, f32[128,1024]{1,0:T(8,128)S(1)}, u32[]{:S(2)}, u32[]{:S(2)}) collective-permute-start(f32[128,1024]{1,0:T(8,128)S(1)} %multiply_subtract_fusion.1), channel_id=1, source_target_pairs={{0,1},{1,0},{2,3},{3,2},{4,5},{5,4},{6,7},{7,6},{8,9},{9,8},{10,11... | collective-permute-start | bytes 1572872 | tf_op jit(solution)/shard_map/ppermute | solution.py:263
  100.8 15.9 %copy-start.6 = (bf16[256,1024]{1,0:T(8,128)(2,1)}, bf16[256,1024]{1,0:T(8,128)(2,1)S(1)}, u32[]{:S(2)}) copy-start(bf16[256,1024]{1,0:T(8,128)(2,1)S(1)} %multiply_convert_fusion.3) | copy-start | bytes 1572868
  100.9 15.9 %copy-start.12 = (f32[256,768]{1,0:T(8,128)S(1)}, f32[256,768]{1,0:T(8,128)}, u32[]{:S(2)}) copy-start(f32[256,768]{1,0:T(8,128)} %copy-done.11) | copy-start | bytes 2359300
  100.9 15.9 %copy-start.16 = (f32[256,256]{1,0:T(8,128)S(1)}, f32[256,256]{1,0:T(8,128)}, u32[]{:S(2)}) copy-start(f32[256,256]{1,0:T(8,128)} %copy-done.15) | copy-start | bytes 786436
  100.9 15.9 %copy-start.40 = (f32[256,256]{1,0:T(8,128)S(1)}, f32[256,256]{1,0:T(8,128)}, u32[]{:S(2)}) copy-start(f32[256,256]{1,0:T(8,128)} %get-tuple-element.88) | copy-start | bytes 786436
  102.4 41.3 %collective-permute-start.33 = (f32[192,1024]{1,0:T(8,128)}, f32[192,1024]{1,0:T(8,128)}, u32[]{:S(2)}, u32[]{:S(2)}) collective-permute-start(f32[192,1024]{1,0:T(8,128)} %collective-permute-done.31.refs_5_), channel_id=1, source_target_pairs={{0,1},{1,0},{2,3},{3,2},{4,5},{5,4},{6,7},{7,6},{8,9},{9,8},{10,11... | collective-permute-start | bytes 2359304 | tf_op jit(solution)/shard_map/ppermute | solution.py:263
  102.6 41.2 %collective-permute-start.26 = (f32[192,1024]{1,0:T(8,128)S(1)}, f32[192,1024]{1,0:T(8,128)}, u32[]{:S(2)}, u32[]{:S(2)}) collective-permute-start(f32[192,1024]{1,0:T(8,128)S(1)} %constant_dynamic-update-slice_fusion.refs_0_), channel_id=1, source_target_pairs={{0,1},{1,0},{2,3},{3,2},{4,5},{5,4},{6,7},{7,6},{8,9},{9,8},{10,11... | collective-permute-start | bytes 2359304 | tf_op jit(solution)/shard_map/ppermute | solution.py:263
  115.1 13.6 %collective-permute-start.17 = (f32[128,1024]{1,0:T(8,128)S(1)}, f32[128,1024]{1,0:T(8,128)}, u32[]{:S(2)}, u32[]{:S(2)}) collective-permute-start(f32[128,1024]{1,0:T(8,128)S(1)} %multiply_subtract_fusion.1), channel_id=1, source_target_pairs={{0,4},{4,0},{8,12},{12,8},{16,20},{20,16},{24,28},{28,24},{1,5},{5... | collective-permute-start | bytes 1572872 | tf_op jit(solution)/shard_map/ppermute | solution.py:266
  116.6 29.2 %collective-permute-start.27 = (f32[192,1024]{1,0:T(8,128)}, f32[192,1024]{1,0:T(8,128)}, u32[]{:S(2)}, u32[]{:S(2)}) collective-permute-start(f32[192,1024]{1,0:T(8,128)} %collective-permute-done.25.refs_1_), channel_id=1, source_target_pairs={{0,1},{1,0},{2,3},{3,2},{4,5},{5,4},{6,7},{7,6},{8,9},{9,8},{10,11... | collective-permute-start | bytes 2359304 | tf_op jit(solution)/shard_map/ppermute | solution.py:263
  117.7 12.3 %copy-start.36 = (bf16[256,256]{1,0:T(8,128)(2,1)}, bf16[256,256]{1,0:T(8,128)(2,1)S(1)}, u32[]{:S(2)}) copy-start(bf16[256,256]{1,0:T(8,128)(2,1)S(1)} %get-tuple-element.83) | copy-start | bytes 393220
  128.6 4.0 %collective-permute-start.18 = (f32[128,1024]{1,0:T(8,128)}, f32[128,1024]{1,0:T(8,128)}, u32[]{:S(2)}, u32[]{:S(2)}) collective-permute-start(f32[128,1024]{1,0:T(8,128)} %collective-permute-done.17), channel_id=1, source_target_pairs={{0,1},{1,0},{2,3},{3,2},{4,5},{5,4},{6,7},{7,6},{8,9},{9,8},{10,11... | collective-permute-start | bytes 1572872 | tf_op jit(solution)/shard_map/ppermute | solution.py:263
  132.6 6.3 %collective-permute-start.6 = (f32[128,1024]{1,0:T(8,128)}, f32[128,1024]{1,0:T(8,128)S(1)}, u32[]{:S(2)}, u32[]{:S(2)}) collective-permute-start(f32[128,1024]{1,0:T(8,128)} %fusion.15), channel_id=1, source_target_pairs={{0,1},{1,0},{2,3},{3,2},{4,5},{5,4},{6,7},{7,6},{8,9},{9,8},{10,11... | collective-permute-start | bytes 1572872 | tf_op jit(solution)/shard_map/ppermute | solution.py:263
  139.3 1.9 collective-permute-start.9
  141.3 28.2 %collective-permute-start.7 = (f32[128,1024]{1,0:T(8,128)S(1)}, f32[128,1024]{1,0:T(8,128)S(1)}, u32[]{:S(2)}, u32[]{:S(2)}) collective-permute-start(f32[128,1024]{1,0:T(8,128)S(1)} %convolution_add_fusion.1), channel_id=1, source_target_pairs={{0,2},{1,3},{2,0},{3,1},{4,6},{5,7},{6,4},{7,5},{8,10},{9,11},{10,... | collective-permute-start | bytes 1572872 | tf_op jit(solution)/shard_map/ppermute | solution.py:274
  142.2 24.3 %collective-permute-start.10 = (f32[128,1024]{1,0:T(8,128)S(1)}, f32[128,1024]{1,0:T(8,128)S(1)}, u32[]{:S(2)}, u32[]{:S(2)}) collective-permute-start(f32[128,1024]{1,0:T(8,128)S(1)} %convolution_add_fusion), channel_id=1, source_target_pairs={{0,2},{1,3},{2,0},{3,1},{4,6},{5,7},{6,4},{7,5},{8,10},{9,11},{10,... | collective-permute-start | bytes 1572872 | tf_op jit(solution)/shard_map/ppermute | solution.py:274
  143.8 54.2 %collective-permute-start.21 = (f32[128,1024]{1,0:T(8,128)S(1)}, f32[128,1024]{1,0:T(8,128)S(1)}, u32[]{:S(2)}, u32[]{:S(2)}) collective-permute-start(f32[128,1024]{1,0:T(8,128)S(1)} %pad_maximum_fusion.7), channel_id=1, source_target_pairs={{0,24},{4,28},{8,0},{12,4},{16,8},{20,12},{24,16},{28,20},{1,25},{... | collective-permute-start | bytes 1572872 | tf_op jit(solution)/shard_map/ppermute | solution.py:269
  143.8 54.3 %collective-permute-start.20 = (f32[128,1024]{1,0:T(8,128)S(1)}, f32[128,1024]{1,0:T(8,128)S(1)}, u32[]{:S(2)}, u32[]{:S(2)}) collective-permute-start(f32[128,1024]{1,0:T(8,128)S(1)} %pad_maximum_fusion.6), channel_id=1, source_target_pairs={{0,16},{4,20},{8,24},{12,28},{16,0},{20,4},{24,8},{28,12},{1,17},{... | collective-permute-start | bytes 1572872 | tf_op jit(solution)/shard_map/ppermute | solution.py:269
  145.8 52.8 %collective-permute-start.19 = (f32[128,1024]{1,0:T(8,128)S(1)}, f32[128,1024]{1,0:T(8,128)S(1)}, u32[]{:S(2)}, u32[]{:S(2)}) collective-permute-start(f32[128,1024]{1,0:T(8,128)S(1)} %pad_maximum_fusion.5), channel_id=1, source_target_pairs={{0,8},{4,12},{8,16},{12,20},{16,24},{20,28},{24,0},{28,4},{1,9},{5... | collective-permute-start | bytes 1572872 | tf_op jit(solution)/shard_map/ppermute | solution.py:269
  147.8 18.7 %copy-start.20 = (f32[256,1024]{1,0:T(8,128)S(1)}, f32[256,1024]{1,0:T(8,128)}, u32[]{:S(2)}) copy-start(f32[256,1024]{1,0:T(8,128)} %copy-done.19) | copy-start | bytes 3145732
  166.7 1.2 collective-permute-start.12
  167.9 48.6 %collective-permute-start.34 = (f32[2,128,1152]{2,1,0:T(8,128)}, f32[2,128,1152]{2,1,0:T(8,128)}, u32[]{:S(2)}, u32[]{:S(2)}) collective-permute-start(f32[2,128,1152]{2,1,0:T(8,128)} %get-tuple-element.48), channel_id=1, source_target_pairs={{0,4},{4,0},{8,12},{12,8},{16,20},{20,16},{24,28},{28,24},{1,5},{5... | collective-permute-start | bytes 3538952 | tf_op jit(solution)/shard_map/ppermute | solution.py:266
  169.5 27.0 %collective-permute-start.13 = (f32[2816]{0:T(1024)S(1)}, f32[2816]{0:T(1024)S(1)}, u32[]{:S(2)}, u32[]{:S(2)}) collective-permute-start(f32[2816]{0:T(1024)S(1)} %pad_maximum_fusion.10), channel_id=1, source_target_pairs={{0,4},{4,0},{8,12},{12,8},{16,20},{20,16},{24,28},{28,24},{1,5},{5... | collective-permute-start | bytes 33800 | tf_op jit(solution)/shard_map/ppermute | solution.py:266
  196.4 14.9 %collective-permute-start.35 = (f32[1152,128]{1,0:T(8,128)}, f32[1152,128]{1,0:T(8,128)S(1)}, u32[]{:S(2)}, u32[]{:S(2)}) collective-permute-start(f32[1152,128]{1,0:T(8,128)} %get-tuple-element.50), channel_id=1, source_target_pairs={{0,4},{4,0},{8,12},{12,8},{16,20},{20,16},{24,28},{28,24},{1,5},{5... | collective-permute-start | bytes 1769480 | tf_op jit(solution)/shard_map/ppermute | solution.py:266
  198.0 14.2 %collective-permute-start.8 = (f32[128,1024]{1,0:T(8,128)S(1)}, f32[128,1024]{1,0:T(8,128)}, u32[]{:S(2)}, u32[]{:S(2)}) collective-permute-start(f32[128,1024]{1,0:T(8,128)S(1)} %add_add_fusion), channel_id=1, source_target_pairs={{0,1},{1,0},{2,3},{3,2},{4,5},{5,4},{6,7},{7,6},{8,9},{9,8},{10,11... | collective-permute-start | bytes 1572872 | tf_op jit(solution)/shard_map/ppermute | solution.py:263
  198.1 3.8 %collective-permute-start.14 = (f32[2816]{0:T(1024)S(1)}, f32[2816]{0:T(1024)S(1)}, u32[]{:S(2)}, u32[]{:S(2)}) collective-permute-start(f32[2816]{0:T(1024)S(1)} %fusion.60), channel_id=1, source_target_pairs={{0,8},{4,12},{8,0},{12,4},{16,24},{20,28},{24,16},{28,20},{1,9},{5... | collective-permute-start | bytes 33800 | tf_op jit(solution)/shard_map/ppermute | solution.py:482
  201.8 4.7 %collective-permute-start.15 = (f32[2816]{0:T(1024)S(1)}, f32[2816]{0:T(1024)S(1)}, u32[]{:S(2)}, u32[]{:S(2)}) collective-permute-start(f32[2816]{0:T(1024)S(1)} %add.272), channel_id=1, source_target_pairs={{0,16},{4,20},{8,24},{12,28},{16,0},{20,4},{24,8},{28,12},{1,17},{... | collective-permute-start | bytes 33800 | tf_op jit(solution)/shard_map/ppermute | solution.py:482
  203.9 10.4 %collective-permute-start.11 = (f32[128,1024]{1,0:T(8,128)S(1)}, f32[128,1024]{1,0:T(8,128)}, u32[]{:S(2)}, u32[]{:S(2)}) collective-permute-start(f32[128,1024]{1,0:T(8,128)S(1)} %multiply_subtract_fusion), channel_id=1, source_target_pairs={{0,1},{1,0},{2,3},{3,2},{4,5},{5,4},{6,7},{7,6},{8,9},{9,8},{10,11... | collective-permute-start | bytes 1572872 | tf_op jit(solution)/shard_map/ppermute | solution.py:263
  (38 other events, 104.7 us)
where the time goes:
time: 221 us; the launch traced here: 220 us
  waiting for transfers between devices  87.7 us (40%)
  starting transfers between devices  49.7 us (22%)
  local copies, waits for them, and re-layouts  25.1 us (11%)
  other arithmetic  22.2 us (10%)
  matrix products  17.4 us (8%)
  Pallas kernels  16.5 us (7%)
    ppermute x5, waiting for transfers between devices, to_side(): return lax.ppermute(values, 'dp', [(i, i ^ 1) for i in range(dp)])  40.6 us
    ppermute x9, starting transfers between devices, to_line(): lax.ppermute(values, 'dp', [(i, (i + 2 * count) % dp) for i in range(dp)])  30.4 us
    ppermute x4, waiting for transfers between devices, over_chips(): lax.ppermute(values, 'tensor', [(i, i ^ stride) for i in range(tensor)])  28 us
    unnamed x109, local copies, waits for them, and re-layouts  20.4 us
    pallas_call x1, Pallas kernels, far_grads(): pl.pallas_call(functools.partial(far_kernel, rows=rows, share=share, bloc...  16.5 us
    ppermute x2, waiting for transfers between devices, gathered(): lax.ppermute(near, 'tensor', [(i, i ^ stride) for i in range(tensor)])  12.2 us
    dot_general x7, matrix products, by_transpose(): lax.dot_general(left, right, (((1,), (1,)), ((), ())), preferred_element_...  6.92 us
    ppermute x5, starting transfers between devices, to_side(): return lax.ppermute(values, 'dp', [(i, i ^ 1) for i in range(dp)])  6.67 us
  transfers between devices with their start and end apart: 36, of which 12 were waited for; matrix products, arithmetic and copies ran while one was open for 22% of the time, Pallas kernels for 8%

commit v1 on v0

--- a/solution.py
+++ b/solution.py
@@ -125,9 +125,63 @@
 
 
 def gathers(dp, tensor, rows, width, hid):
-    powers = all(size > 1 and size & (size - 1) == 0 for size in (dp, tensor))
+    powers = tensor == 4 and dp > 2 and dp & (dp - 1) == 0
     whole = rows % (8 * tensor) == 0 and hid % (128 * tensor) == 0
     return powers and whole and width % (128 * dp) == 0 and dp * rows <= 2 * width
+
+
+def join_kernel(*refs):
+    start = 0
+    for ref in refs[:-1]:
+        refs[-1][start : start + ref.shape[0]] = ref[...]
+        start += ref.shape[0]
+
+
+def join(pieces):
+    rows = sum(piece.shape[0] for piece in pieces)
+    return pl.pallas_call(
+        join_kernel,
+        out_shape=jax.ShapeDtypeStruct((rows, *pieces[0].shape[1:]), pieces[0].dtype),
+        compiler_params=pltpu.CompilerParams(vmem_limit_bytes=4 << 20),
+        cost_estimate=pl.CostEstimate(
+            flops=0, bytes_accessed=2 * rows * pieces[0].shape[1] * 4, transcendentals=0
+        ),
+        name="join",
+    )(*pieces)
+
+
+def conv_kernel(at_block, *refs, block):
+    first, second, refs = refs[:4], refs[4:8], refs[8:]
+    for k, out in enumerate(refs):
+        at = pl.ds(pl.multiple_of(at_block[k] * block, block), block)
+        split = first[2].shape[1]
+        out[:, :split] = cross(first[0][:, at], first[2][...]) + cross(
+            second[0][:, at], second[2][...]
+        )
+        out[:, split:] = cross(first[1][:, at], first[3][...]) + cross(
+            second[1][:, at], second[3][...]
+        )
+
+
+def conv_parts(at_block, first, second, line, block):
+    rows, chans = first[3].shape
+    return pl.pallas_call(
+        functools.partial(conv_kernel, block=block),
+        out_shape=[jax.ShapeDtypeStruct((block, 4 * chans), jnp.float32)] * line,
+        grid_spec=pltpu.PrefetchScalarGridSpec(
+            num_scalar_prefetch=1,
+            grid=(),
+            in_specs=[pl.BlockSpec(memory_space=pltpu.VMEM)] * 8,
+            out_specs=[pl.BlockSpec(memory_space=pltpu.VMEM)] * line,
+        ),
+        compiler_params=pltpu.CompilerParams(vmem_limit_bytes=16 << 20),
+        cost_estimate=pl.CostEstimate(
+            flops=16 * rows * line * block * chans,
+            bytes_accessed=16 * rows * (line * 2 * block + 2 * chans),
+            transcendentals=0,
+        ),
+        name="conv_parts",
+    )(at_block, *first, *second)
 
 
 def far_kernel(
@@ -137,9 +191,11 @@
     share,
     block,
 ):
-    pieces, refs = refs[:8], refs[8:]
+    normed, cots, refs = refs[:4], refs[4:8], refs[8:]
     norm, x_near, c_near, h_near, dg_near, du_near, wg, wu, wd = refs[:9]
-    gu_own, gu_there, down_own, down_there, x_all, c_all, xs, cs, dg, du, hidden = refs[9:]
+    gu_own, gu_there, down_own, down_there = refs[9:13]
+    x_all, c_all, xs, cs, w_both, d_both, hidden = refs[13:]
+    step = wd.shape[0]
     f32, bf16 = jnp.float32, jnp.bfloat16
 
     @pl.when(pl.program_id(0) == 0)
@@ -148,37 +204,39 @@
         c_all[:rows] = c_near[...]
         for i in range(4):
             at = pl.ds(rows + i * share, share)
-            x_all[at] = (pieces[i][...] * norm[...]).astype(bf16)
-            c_all[at] = pieces[4 + i][...].astype(bf16)
+            x_all[at] = (normed[i][...] * norm[...]).astype(bf16)
+            c_all[at] = cots[i][...].astype(bf16)
         for i in range(2):
             at = pl.ds(pl.multiple_of(where[i] * block, block), block)
             xs[:, i * block : (i + 1) * block] = x_all[:, at]
             cs[:, i * block : (i + 1) * block] = c_all[:, at]
 
-    act = jnp.dot(x_all[rows:], wg[...], preferred_element_type=f32)
-    up = jnp.dot(x_all[rows:], wu[...], preferred_element_type=f32)
+    w_both[:, :step] = wg[...]
+    w_both[:, step:] = wu[...]
+    hidden[:rows] = h_near[...]
+    d_both[:rows, :step] = dg_near[...]
+    d_both[:rows, step:] = du_near[...]
+    acts = jnp.dot(x_all[rows:], w_both[...], preferred_element_type=f32)
+    act, up = acts[:, :step], acts[:, step:]
     d_hidden = by_transpose(c_all[rows:], wd[...])
     sig = jax.nn.sigmoid(act)
-    hidden[:rows] = h_near[...]
-    dg[:rows] = dg_near[...]
-    du[:rows] = du_near[...]
-    hidden[rows:] = (act * sig * up).astype(bf16)
-    dg[rows:] = (d_hidden * up * sig * (1.0 + act * (1.0 - sig))).astype(bf16)
-    du[rows:] = (d_hidden * act * sig).astype(bf16)
-    for i, grad in enumerate((dg, du)):
-        both = cross(xs[...], grad[...])
-        gu_own[i] = both[:block]
-        gu_there[i] = both[block:]
+    product = act * sig
+    hidden[rows:] = (product * up).astype(bf16)
+    d_both[rows:, :step] = (d_hidden * up * sig * (1.0 + act * (1.0 - sig))).astype(bf16)
+    d_both[rows:, step:] = (d_hidden * product).astype(bf16)
+    both = cross(xs[...], d_both[...])
+    for i in range(2):
+        gu_own[i] = both[:block, i * step : (i + 1) * step]
+        gu_there[i] = both[block:, i * step : (i + 1) * step]
     both = cross(hidden[...], cs[...])
     down_own[...] = both[:, :block]
     down_there[...] = both[:, block:]
 
 
-def far_grads(where, pieces, norm, x_near, c_near, h_near, d_gu_near, w_gu, w_down):
+def far_grads(where, block, normed, cots, norm, x_near, c_near, h_near, d_gu_near, w_gu, w_down):
     rows, width = x_near.shape
     hid = w_down.shape[0]
-    share = pieces[0].shape[0]
-    block = 128
+    share = normed[0].shape[0]
     tokens = rows + 4 * share
     step = max(size for size in range(128, 513, 128) if hid % size == 0)
     steps = hid // step
@@ -199,7 +257,7 @@
             num_scalar_prefetch=1,
             grid=(steps,),
             in_specs=[
-                *[whole(piece) for piece in pieces],
+                *[whole(piece) for piece in (*normed, *cots)],
                 whole(norm),
                 whole(x_near),
                 whole(c_near),
@@ -217,17 +275,19 @@
             scratch_shapes=[
                 *[pltpu.VMEM((tokens, width), bf16)] * 2,
                 *[pltpu.VMEM((tokens, 2 * block), bf16)] * 2,
-                *[pltpu.VMEM((tokens, step), bf16)] * 3,
+                pltpu.VMEM((width, 2 * step), bf16),
+                pltpu.VMEM((tokens, 2 * step), bf16),
+                pltpu.VMEM((tokens, step), bf16),
             ],
         ),
-        compiler_params=pltpu.CompilerParams(vmem_limit_bytes=48 << 20),
+        compiler_params=pltpu.CompilerParams(vmem_limit_bytes=52 << 20),
         cost_estimate=pl.CostEstimate(
-            flops=2 * hid * (3 * 4 * share * width + 3 * tokens * 2 * block),
-            bytes_accessed=8 * share * width * 4 + 6 * hid * width + 24 * hid * block,
-            transcendentals=4 * share * hid,
+            flops=6 * hid * (tokens - rows) * width + 12 * hid * tokens * block,
+            bytes_accessed=8 * (tokens - rows) * width + 6 * hid * width + 24 * hid * block,
+            transcendentals=(tokens - rows) * hid,
         ),
         name="far_grads",
-    )(where, *pieces, norm, x_near, c_near, h_near, d_gu_near, d_gu_near, w_gu, w_gu, w_down)
+    )(where, *normed, *cots, norm, x_near, c_near, h_near, d_gu_near, d_gu_near, w_gu, w_gu, w_down)
 
 
 def body_gather(
@@ -298,17 +358,15 @@
 
     chip = lax.axis_index("tensor") // 2
 
-    def spread(quarter):
-        return [to_line(quarter, k) for k in range(1, line)]
+    def along_line(values):
+        return [to_line(values, k) for k in range(1, line)]
+
+    def quarter(values, start):
+        return lax.dynamic_slice_in_dim(values, start + chip * share, share, 0)
 
     def gathered(pieces):
-        near = jnp.concatenate(pieces, axis=0)
-        stride = 2
-        while stride < tensor:
-            there = lax.ppermute(near, "tensor", [(i, i ^ stride) for i in range(tensor)])
-            stride *= 2
-            if stride < tensor:
-                near = jnp.concatenate([near, there], axis=0)
+        near = join(pieces)
+        there = lax.ppermute(near, "tensor", [(i, i ^ 2) for i in range(tensor)])
         return near, there, to_core(near), to_core(there)
 
     def conv_forward(tok):
@@ -367,8 +425,7 @@
         mine(gated), other(gated), lambda part: jnp.dot(part, w_out, preferred_element_type=f32)
     )
 
-    cot_quarter = lax.dynamic_slice_in_dim(cotangent, core * half + chip * share, share, 0)
-    cot_pieces = spread(cot_quarter.astype(f32))
+    cot_pieces = along_line(quarter(cotangent, core * half).astype(f32))
     w_gu_flat = after(w_gate_up, gated).reshape(width, 2 * hid)
     mix_there, w_gu_flat = lax.optimization_barrier((mix_there, w_gu_flat))
     beside = to_side(after(tokens, gated).astype(f32))
@@ -377,8 +434,8 @@
     s2 = lax.rsqrt(jnp.mean(resid * resid, axis=-1, keepdims=True) + eps)
     scaled = resid * s2
     scaled_there = to_core(scaled)
-    normed2_pieces = spread(lax.dynamic_slice_in_dim(scaled, chip * share, share, 0))
-    cot_far = gathered([after(p, scaled) for p in cot_pieces])
+    normed2_pieces = along_line(quarter(scaled, 0))
+    cot_far = gathered([after(piece, scaled) for piece in cot_pieces])
     normed2_near = (jnp.concatenate([scaled, scaled_there], axis=0) * norm_second).astype(
         bf16
     )
@@ -409,37 +466,25 @@
     d_resid_beside = after(d_resid_beside, d_proj)
     d_resid_next = ordered(d_resid_beside, to_core(d_resid_beside)).astype(bf16)
     d_proj_beside, _ = conv_backward(d_resid_next, saved_beside)
-    both = [
-        jnp.concatenate(pair, axis=0)
-        for pair in (
-            (normed1, saved_beside[1]),
-            (d_resid_seq, d_resid_next),
-            (d_proj, d_proj_beside),
-            (gated, saved_beside[7]),
-        )
-    ]
-
-    def columns(values, start):
-        return lax.dynamic_slice_in_dim(values, start, block, 1)
-
-    def conv_part(k):
-        start = (lax.rem(along + k, line) * 2 + side) * block
-        grads = jnp.concatenate(
-            [cross(columns(both[0], start), both[2]), cross(columns(both[1], start), both[3])],
-            axis=1,
-        )
-        return grads
-
-    parts = [to_line(conv_part(k), k) for k in range(1, line)]
-    kept = conv_part(0)
+
+    kept, *parts = conv_parts(
+        lax.rem(along + jnp.arange(line, dtype=jnp.int32), line) * 2 + side,
+        (normed1, d_resid_seq, d_proj, gated),
+        (saved_beside[1], d_resid_next, d_proj_beside, saved_beside[7]),
+        line,
+        block,
+    )
+    parts = [to_line(part, k + 1) for k, part in enumerate(parts)]
     total = sum(parts, kept)
     grad_in = total[:, : 3 * chans].reshape(block, 3, chans)
     grad_out = total[:, 3 * chans :].T
 
-    normed2_far = gathered([after(p, d_normed2_chip) for p in normed2_pieces])
+    normed2_far = gathered([after(piece, d_resid) for piece in normed2_pieces])
     gu_here, gu_there, down_here, down_there = far_grads(
         jnp.stack([place, along * 2 + 1 - side]),
-        (*normed2_far, *cot_far),
+        block,
+        normed2_far,
+        cot_far,
         norm_second.reshape(1, width),
         normed2_near,
         cot_near,
@@ -448,10 +493,10 @@
         w_gu_flat,
         w_down,
     )
+    gu_there = to_side(gu_there)
     down_there = to_side(down_there)
-    gu_there = to_side(gu_there)
+    grad_gu = (gu_here + gu_there).swapaxes(0, 1)
     grad_down = down_here + down_there
-    grad_gu = (gu_here + gu_there).swapaxes(0, 1)
 
     d_normed1 = d_normed1 + d_normed1_there
     xf_mine, s1_mine = mine(xf), mine(s1)
@@ -476,12 +521,12 @@
     gains = jnp.concatenate([gn1, gn2])
     gains = gains + to_core(gains)
     small = jnp.concatenate([gains, gtaps.reshape(-1)])
-    small = small + to_side(small)
     stride = 2
     while stride < dp:
         there = lax.ppermute(small, "dp", [(i, i ^ stride) for i in range(dp)])
         small = small + there
         stride *= 2
+    small = small + to_side(small)
     return (
         block_out,
         grad_tokens,

time: 221 us -> 245 us (1.11)
  waiting for transfers between devices: 87.7 us -> 108 us
  local copies, waits for them, and re-layouts: 25.1 us -> 19.2 us
  other arithmetic: 22.2 us -> 27.4 us
  matrix products: 17.4 us -> 20.8 us
    ppermute x9, waiting for transfers between devices: 0.35 us -> 24.9 us  [to_line(): lax.ppermute(values, 'dp', [(i, (i + 2 * count) % dp) for i in range(dp)])]
    ppermute x5, waiting for transfers between devices: 40.6 us -> 30.9 us  [to_side(): return lax.ppermute(values, 'dp', [(i, i ^ 1) for i in range(dp)])]
    ppermute x4, waiting for transfers between devices: 28 us -> 36.7 us  [over_chips(): lax.ppermute(values, 'tensor', [(i, i ^ stride) for i in range(tensor)])]
    unnamed x109 -> x117, local copies, waits for them, and re-layouts: 20.4 us -> 14.2 us
    dot_general x7, matrix products: 6.92 us -> 12.4 us  [by_transpose(): lax.dot_general(left, right, (((1,), (1,)), ((), ())), preferred_element_...]
    ppermute x2, waiting for transfers between devices: 12.2 us -> 9.45 us  [gathered(): there = lax.ppermute(near, 'tensor', [(i, i ^ 2) for i in range(tensor)])]
    ppermute x9, starting transfers between devices: 30.4 us -> 27.8 us  [to_line(): lax.ppermute(values, 'dp', [(i, (i + 2 * count) % dp) for i in range(dp)])]
  transfers between devices with their start and end apart: 36 -> 36, of which waited for: 12 -> 12; matrix products, arithmetic and copies ran while one was open for 22% -> 21% of each run, Pallas kernels for 8% -> 8%
where the time goes in v1:
time: 245 us; the launch traced here: 244 us
  waiting for transfers between devices  108 us (44%)
  starting transfers between devices  48.7 us (20%)
  other arithmetic  27.4 us (11%)
  matrix products  20.8 us (8%)
  local copies, waits for them, and re-layouts  19.2 us (8%)
  Pallas kernels  18.4 us (8%)
    ppermute x4, waiting for transfers between devices, over_chips(): lax.ppermute(values, 'tensor', [(i, i ^ stride) for i in range(tensor)])  36.7 us
    ppermute x5, waiting for transfers between devices, to_side(): return lax.ppermute(values, 'dp', [(i, i ^ 1) for i in range(dp)])  30.9 us
    ppermute x9, starting transfers between devices, to_line(): lax.ppermute(values, 'dp', [(i, (i + 2 * count) % dp) for i in range(dp)])  27.8 us
    ppermute x9, waiting for transfers between devices, to_line(): lax.ppermute(values, 'dp', [(i, (i + 2 * count) % dp) for i in range(dp)])  24.9 us
    pallas_call x1, Pallas kernels, far_grads(): pl.pallas_call(functools.partial(far_kernel, rows=rows, share=share, bloc...  16.1 us
    unnamed x117, local copies, waits for them, and re-layouts  14.2 us
    dot_general x7, matrix products, by_transpose(): lax.dot_general(left, right, (((1,), (1,)), ((), ())), preferred_element_...  12.4 us
    ppermute x2, waiting for transfers between devices, gathered(): there = lax.ppermute(near, 'tensor', [(i, i ^ 2) for i in range(tensor)])  9.45 us
  transfers between devices with their start and end apart: 36, of which 12 were waited for; matrix products, arithmetic and copies ran while one was open for 21% of the time, Pallas kernels for 8%

profile of v1, /device:TPU:0, one launch (start us, length us, event | category | flops | bytes accessed | tf_op | source)
XLA Modules:
  0.0 244.3 jit_solution(13194297456215014708)
XLA Ops:
  2.0 1.8 copy.23
  5.8 1.9 multiply_convert_fusion.12
  8.5 1.5 collective-permute-done
  10.2 2.9 %collective-permute-start.1 = (f32[128,1024]{1,0:T(8,128)S(1)}, f32[128,1024]{1,0:T(8,128)}, u32[]{:S(2)}, u32[]{:S(2)}) collective-permute-start(f32[128,1024]{1,0:T(8,128)S(1)} %convolution_add_fusion.3), channel_id=1, source_target_pairs={{0,2},{1,3},{2,0},{3,1},{4,6},{5,7},{6,4},{7,5},{8,10},{9,11},{10,... | collective-permute-start | bytes 1572872 | tf_op jit(solution)/shard_map/ppermute | solution.py:334
  13.3 5.7 %copy.31 = bf16[128,8,2,1152]{3,1,2,0:T(8,128)(2,1)} copy(bf16[128,8,2,1152]{3,2,1,0:T(2,128)(2,1)} %bitcast.62) | data formatting | bytes 9437184
  19.0 6.5 %collective-permute-done.1 = f32[128,1024]{1,0:T(8,128)} collective-permute-done((f32[128,1024]{1,0:T(8,128)S(1)}, f32[128,1024]{1,0:T(8,128)}, u32[]{:S(2)}, u32[]{:S(2)}) %collective-permute-start.1) | collective-permute-done | bytes 524320 | tf_op jit(solution)/shard_map/ppermute | solution.py:334
  27.9 1.6 dynamic-slice_convert_fusion
  29.5 1.8 collective-permute-start.28
  31.3 2.6 %collective-permute-start.29 = (f32[64,1024]{1,0:T(8,128)}, f32[64,1024]{1,0:T(8,128)S(1)}, u32[]{:S(2)}, u32[]{:S(2)}) collective-permute-start(f32[64,1024]{1,0:T(8,128)} %dynamic-slice_convert_fusion), channel_id=1, source_target_pairs={{0,16},{4,20},{8,24},{12,28},{16,0},{20,4},{24,8},{28,12},{1,17},{... | collective-permute-start | bytes 786440 | tf_op jit(solution)/shard_map/ppermute | solution.py:329
  33.9 1.3 collective-permute-start.30
  36.5 1.5 collective-permute-start.16
  40.6 1.4 fusion.refs_9_
  42.1 3.9 %fusion.26 = f32[256,2304]{1,0:T(8,128)S(1)} fusion(bf16[256,1024]{1,0:T(8,128)(2,1)S(1)} %fusion.refs_9_, bf16[1024,2304]{1,0:T(8,128)(2,1)} %bitcast.47), kind=kOutput, calls=%fused_computation.109 | convolution fusion | flops 1207959552 | bytes 7602176 | tf_op jit(solution)/shard_map/dot_general | solution.py:412
  46.0 2.2 multiply_convert_fusion
  48.1 2.4 fusion.3
  53.0 6.6 %collective-permute-start.24 = (f32[64,1024]{1,0:T(8,128)S(1)}, f32[64,1024]{1,0:T(8,128)S(1)}, u32[]{:S(2)}, u32[]{:S(2)}) collective-permute-start(f32[64,1024]{1,0:T(8,128)S(1)} %constant_dynamic-slice_fusion), channel_id=1, source_target_pairs={{0,24},{4,28},{8,0},{12,4},{16,8},{20,12},{24,16},{28,20},{1,25},{... | collective-permute-start | bytes 786440 | tf_op jit(solution)/shard_map/ppermute | solution.py:329
  59.7 4.3 %convolution_add_fusion.2 = f32[128,1024]{1,0:T(8,128)S(1)} fusion(f32[128,1024]{1,0:T(8,128)} %collective-permute-done.3, bf16[128,2304]{1,0:T(8,128)(2,1)S(1)} %fusion.1, bf16[1024,2304]{1,0:T(8,128)(2,1)} %bitcast.48), kind=kOutput, calls=%fused_computation.7 | convolution fusion | flops 604110848 | bytes 6356992 | tf_op jit(solution)/shard_map/dot_general | solution.py:31
  64.0 1.6 collective-permute-start.4
  67.2 1.4 multiply_reduce_fusion
  68.6 10.3 %collective-permute-done.4 = f32[128,1024]{1,0:T(8,128)S(1)} collective-permute-done((f32[128,1024]{1,0:T(8,128)S(1)}, f32[128,1024]{1,0:T(8,128)S(1)}, u32[]{:S(2)}, u32[]{:S(2)}) %collective-permute-start.4) | collective-permute-done | bytes 524320 | tf_op jit(solution)/shard_map/ppermute | solution.py:334
  80.0 1.7 multiply_convert_fusion.3.refs_4_
  81.7 1.6 fusion.27
  83.5 9.4 %collective-permute-done.31.refs_5_ = f32[192,1024]{1,0:T(8,128)} collective-permute-done((f32[192,1024]{1,0:T(8,128)S(1)}, f32[192,1024]{1,0:T(8,128)}, u32[]{:S(2)}, u32[]{:S(2)}) %collective-permute-start.31) | collective-permute-done | bytes 786464 | tf_op jit(solution)/shard_map/ppermute | solution.py:369
  93.0 1.5 collective-permute-start.17
  95.5 1.5 collective-permute-start.25
  99.4 8.0 %collective-permute-done.17 = f32[128,1024]{1,0:T(8,128)} collective-permute-done((f32[128,1024]{1,0:T(8,128)S(1)}, f32[128,1024]{1,0:T(8,128)}, u32[]{:S(2)}, u32[]{:S(2)}) %collective-permute-start.17) | collective-permute-done | bytes 524320 | tf_op jit(solution)/shard_map/ppermute | solution.py:326
  107.4 1.3 fusion.5
  110.8 1.3 add_convert_fusion.1
  112.1 1.6 convolution_add_fusion
  114.1 1.6 collective-permute-start.10
  117.9 10.4 %collective-permute-done.10 = f32[128,1024]{1,0:T(8,128)S(1)} collective-permute-done((f32[128,1024]{1,0:T(8,128)S(1)}, f32[128,1024]{1,0:T(8,128)S(1)}, u32[]{:S(2)}, u32[]{:S(2)}) %collective-permute-start.10) | collective-permute-done | bytes 524320 | tf_op jit(solution)/shard_map/ppermute | solution.py:334
  128.3 1.5 collective-permute-start.7
  129.9 1.3 conv_parts.1
  132.0 9.6 %collective-permute-done.7 = f32[128,1024]{1,0:T(8,128)S(1)} collective-permute-done((f32[128,1024]{1,0:T(8,128)S(1)}, f32[128,1024]{1,0:T(8,128)S(1)}, u32[]{:S(2)}, u32[]{:S(2)}) %collective-permute-start.7) | collective-permute-done | bytes 524320 | tf_op jit(solution)/shard_map/ppermute | solution.py:334
  141.5 11.2 %collective-permute-start.21 = (f32[128,1024]{1,0:T(8,128)S(1)}, f32[128,1024]{1,0:T(8,128)S(1)}, u32[]{:S(2)}, u32[]{:S(2)}) collective-permute-start(f32[128,1024]{1,0:T(8,128)S(1)} %get-tuple-element.48), channel_id=1, source_target_pairs={{0,24},{4,28},{8,0},{12,4},{16,8},{20,12},{24,16},{28,20},{1,25},{... | collective-permute-start | bytes 1572872 | tf_op jit(solution)/shard_map/ppermute | solution.py:329
  154.2 1.7 collective-permute-start.19
  157.1 16.1 %far_grads.1 = (f32[2,128,1152]{2,1,0:T(8,128)}, f32[2,128,1152]{2,1,0:T(8,128)}, f32[1152,128]{1,0:T(8,128)S(1)}, f32[1152,128]{1,0:T(8,128)}) custom-call(s32[2]{0:T(128)S(1)} %pad_add_fusion.where, f32[192,1024]{1,0:T(8,128)} %join.2.refs_0_, f32[192,1024]{1,0:T(8,128)} %collective-permute-done.25.refs_1_, f32[192,1024]{1,0:T(8,128)} %copy-done.52, ...), custom_call_target="tpu_custom_call" | custom-call | flops 7247757312 | bytes 16908288 | tf_op jit(solution)/shard_map/far_grads/pallas_call | solution.py:250
  173.1 24.9 %collective-permute-done.20 = f32[128,1024]{1,0:T(8,128)S(1)} collective-permute-done((f32[128,1024]{1,0:T(8,128)S(1)}, f32[128,1024]{1,0:T(8,128)S(1)}, u32[]{:S(2)}, u32[]{:S(2)}) %collective-permute-start.20) | collective-permute-done | bytes 524320 | tf_op jit(solution)/shard_map/ppermute | solution.py:329
  198.3 1.8 collective-permute-start.34
  200.1 1.9 collective-permute-done.13
  202.0 1.8 collective-permute-start.14
  204.0 2.6 %collective-permute-done.14 = f32[2816]{0:T(1024)S(1)} collective-permute-done((f32[2816]{0:T(1024)S(1)}, f32[2816]{0:T(1024)S(1)}, u32[]{:S(2)}, u32[]{:S(2)}) %collective-permute-start.14) | collective-permute-done | bytes 11296 | tf_op jit(solution)/shard_map/ppermute | solution.py:526
  206.6 1.7 collective-permute-start.15
  210.6 17.1 %collective-permute-done.15 = f32[2816]{0:T(1024)S(1)} collective-permute-done((f32[2816]{0:T(1024)S(1)}, f32[2816]{0:T(1024)S(1)}, u32[]{:S(2)}, u32[]{:S(2)}) %collective-permute-start.15) | collective-permute-done | bytes 11296 | tf_op jit(solution)/shard_map/ppermute | solution.py:326
  233.2 5.8 %collective-permute-done.35 = f32[1152,128]{1,0:T(8,128)} collective-permute-done((f32[1152,128]{1,0:T(8,128)}, f32[1152,128]{1,0:T(8,128)}, u32[]{:S(2)}, u32[]{:S(2)}) %collective-permute-start.35) | collective-permute-done | bytes 589856 | tf_op jit(solution)/shard_map/ppermute | solution.py:326
  239.0 1.9 add.269
  240.9 1.4 add_bitcast_fusion
  242.3 1.9 copy.29
  (229 shorter events, 35.3 us)
Async XLA Ops:
  7.9 2.1 collective-permute-start
  10.2 15.2 %collective-permute-start.1 = (f32[128,1024]{1,0:T(8,128)S(1)}, f32[128,1024]{1,0:T(8,128)}, u32[]{:S(2)}, u32[]{:S(2)}) collective-permute-start(f32[128,1024]{1,0:T(8,128)S(1)} %convolution_add_fusion.3), channel_id=1, source_target_pairs={{0,2},{1,3},{2,0},{3,1},{4,6},{5,7},{6,4},{7,5},{8,10},{9,11},{10,... | collective-permute-start | bytes 1572872 | tf_op jit(solution)/shard_map/ppermute | solution.py:334
  27.4 13.2 %collective-permute-start.2 = (f32[128,1024]{1,0:T(8,128)S(1)}, f32[128,1024]{1,0:T(8,128)}, u32[]{:S(2)}, u32[]{:S(2)}) collective-permute-start(f32[128,1024]{1,0:T(8,128)S(1)} %broadcast_multiply_fusion), channel_id=1, source_target_pairs={{0,1},{1,0},{2,3},{3,2},{4,5},{5,4},{6,7},{7,6},{8,9},{9,8},{10,11... | collective-permute-start | bytes 1572872 | tf_op jit(solution)/shard_map/ppermute | solution.py:323
  29.5 22.2 %collective-permute-start.28 = (f32[64,1024]{1,0:T(8,128)}, f32[64,1024]{1,0:T(8,128)S(1)}, u32[]{:S(2)}, u32[]{:S(2)}) collective-permute-start(f32[64,1024]{1,0:T(8,128)} %dynamic-slice_convert_fusion), channel_id=1, source_target_pairs={{0,8},{4,12},{8,16},{12,20},{16,24},{20,28},{24,0},{28,4},{1,9},{5... | collective-permute-start | bytes 786440 | tf_op jit(solution)/shard_map/ppermute | solution.py:329
  31.3 21.1 %collective-permute-start.29 = (f32[64,1024]{1,0:T(8,128)}, f32[64,1024]{1,0:T(8,128)S(1)}, u32[]{:S(2)}, u32[]{:S(2)}) collective-permute-start(f32[64,1024]{1,0:T(8,128)} %dynamic-slice_convert_fusion), channel_id=1, source_target_pairs={{0,16},{4,20},{8,24},{12,28},{16,0},{20,4},{24,8},{28,12},{1,17},{... | collective-permute-start | bytes 786440 | tf_op jit(solution)/shard_map/ppermute | solution.py:329
  33.9 19.1 %collective-permute-start.30 = (f32[64,1024]{1,0:T(8,128)}, f32[64,1024]{1,0:T(8,128)S(1)}, u32[]{:S(2)}, u32[]{:S(2)}) collective-permute-start(f32[64,1024]{1,0:T(8,128)} %dynamic-slice_convert_fusion), channel_id=1, source_target_pairs={{0,24},{4,28},{8,0},{12,4},{16,8},{20,12},{24,16},{28,20},{1,25},{... | collective-permute-start | bytes 786440 | tf_op jit(solution)/shard_map/ppermute | solution.py:329
  36.5 30.2 %collective-permute-start.16 = (f32[256,1024]{1,0:T(8,128)}, f32[256,1024]{1,0:T(8,128)}, u32[]{:S(2)}, u32[]{:S(2)}) collective-permute-start(f32[256,1024]{1,0:T(8,128)} %convert_element_type.46), channel_id=1, source_target_pairs={{0,4},{4,0},{8,12},{12,8},{16,20},{20,16},{24,28},{28,24},{1,5},{5... | collective-permute-start | bytes 3145736 | tf_op jit(solution)/shard_map/ppermute | solution.py:326
  50.6 9.1 %collective-permute-start.3 = (f32[128,1024]{1,0:T(8,128)}, f32[128,1024]{1,0:T(8,128)}, u32[]{:S(2)}, u32[]{:S(2)}) collective-permute-start(f32[128,1024]{1,0:T(8,128)} %fusion.3), channel_id=1, source_target_pairs={{0,1},{1,0},{2,3},{3,2},{4,5},{5,4},{6,7},{7,6},{8,9},{9,8},{10,11... | collective-permute-start | bytes 1572872 | tf_op jit(solution)/shard_map/ppermute | solution.py:323
  51.8 31.5 %collective-permute-start.22 = (f32[64,1024]{1,0:T(8,128)S(1)}, f32[64,1024]{1,0:T(8,128)S(1)}, u32[]{:S(2)}, u32[]{:S(2)}) collective-permute-start(f32[64,1024]{1,0:T(8,128)S(1)} %constant_dynamic-slice_fusion), channel_id=1, source_target_pairs={{0,8},{4,12},{8,16},{12,20},{16,24},{20,28},{24,0},{28,4},{1,9},{5... | collective-permute-start | bytes 786440 | tf_op jit(solution)/shard_map/ppermute | solution.py:329
  52.5 40.5 %collective-permute-start.23 = (f32[64,1024]{1,0:T(8,128)S(1)}, f32[64,1024]{1,0:T(8,128)S(1)}, u32[]{:S(2)}, u32[]{:S(2)}) collective-permute-start(f32[64,1024]{1,0:T(8,128)S(1)} %constant_dynamic-slice_fusion), channel_id=1, source_target_pairs={{0,16},{4,20},{8,24},{12,28},{16,0},{20,4},{24,8},{28,12},{1,17},{... | collective-permute-start | bytes 786440 | tf_op jit(solution)/shard_map/ppermute | solution.py:329
  53.0 41.5 %collective-permute-start.24 = (f32[64,1024]{1,0:T(8,128)S(1)}, f32[64,1024]{1,0:T(8,128)S(1)}, u32[]{:S(2)}, u32[]{:S(2)}) collective-permute-start(f32[64,1024]{1,0:T(8,128)S(1)} %constant_dynamic-slice_fusion), channel_id=1, source_target_pairs={{0,24},{4,28},{8,0},{12,4},{16,8},{20,12},{24,16},{28,20},{1,25},{... | collective-permute-start | bytes 786440 | tf_op jit(solution)/shard_map/ppermute | solution.py:329
  59.6 23.7 %copy-start.1 = (f32[192,1024]{1,0:T(8,128)}, f32[192,1024]{1,0:T(8,128)S(1)}, u32[]{:S(2)}) copy-start(f32[192,1024]{1,0:T(8,128)S(1)} %join.3.refs_4_) | copy-start | bytes 2359300
  64.0 14.9 %copy-start.8 = (f32[128,1024]{1,0:T(8,128)S(1)}, f32[128,1024]{1,0:T(8,128)}, u32[]{:S(2)}) copy-start(f32[128,1024]{1,0:T(8,128)} %copy-done.7) | copy-start | bytes 1572868
  64.0 14.9 %copy-start.48 = (f32[128]{0:T(128)S(1)}, f32[128]{0:T(128)}, u32[]{:S(2)}) copy-start(f32[128]{0:T(128)} %copy-done.47) | copy-start | bytes 1540
  64.0 14.9 %collective-permute-start.4 = (f32[128,1024]{1,0:T(8,128)S(1)}, f32[128,1024]{1,0:T(8,128)S(1)}, u32[]{:S(2)}, u32[]{:S(2)}) collective-permute-start(f32[128,1024]{1,0:T(8,128)S(1)} %convolution_add_fusion.2), channel_id=1, source_target_pairs={{0,2},{1,3},{2,0},{3,1},{4,6},{5,7},{6,4},{7,5},{8,10},{9,11},{10,... | collective-permute-start | bytes 1572872 | tf_op jit(solution)/shard_map/ppermute | solution.py:334
  66.7 26.3 %collective-permute-start.31 = (f32[192,1024]{1,0:T(8,128)S(1)}, f32[192,1024]{1,0:T(8,128)}, u32[]{:S(2)}, u32[]{:S(2)}) collective-permute-start(f32[192,1024]{1,0:T(8,128)S(1)} %join.3.refs_4_), channel_id=1, source_target_pairs={{0,2},{1,3},{2,0},{3,1},{4,6},{5,7},{6,4},{7,5},{8,10},{9,11},{10,... | collective-permute-start | bytes 2359304 | tf_op jit(solution)/shard_map/ppermute | solution.py:369
  79.9 17.1 %copy-start.24 = (f32[128,1024]{1,0:T(8,128)}, f32[128,1024]{1,0:T(8,128)S(1)}, u32[]{:S(2)}) copy-start(f32[128,1024]{1,0:T(8,128)S(1)} %multiply_subtract_fusion.1) | copy-start | bytes 1572868
  79.9 17.1 %collective-permute-start.5 = (f32[128,1024]{1,0:T(8,128)S(1)}, f32[128,1024]{1,0:T(8,128)S(1)}, u32[]{:S(2)}, u32[]{:S(2)}) collective-permute-start(f32[128,1024]{1,0:T(8,128)S(1)} %multiply_subtract_fusion.1), channel_id=1, source_target_pairs={{0,1},{1,0},{2,3},{3,2},{4,5},{5,4},{6,7},{7,6},{8,9},{9,8},{10,11... | collective-permute-start | bytes 1572872 | tf_op jit(solution)/shard_map/ppermute | solution.py:323
  83.3 13.9 %copy-start.11 = (f32[256,768]{1,0:T(8,128)S(1)}, f32[256,768]{1,0:T(8,128)}, u32[]{:S(2)}) copy-start(f32[256,768]{1,0:T(8,128)} %copy-done.10) | copy-start | bytes 2359300
  83.3 13.9 %copy-start.15 = (f32[256,256]{1,0:T(8,128)S(1)}, f32[256,256]{1,0:T(8,128)}, u32[]{:S(2)}) copy-start(f32[256,256]{1,0:T(8,128)} %slice_multiply_fusion.2) | copy-start | bytes 786436
  83.3 13.9 %copy-start.34 = (f32[256,256]{1,0:T(8,128)S(1)}, f32[256,256]{1,0:T(8,128)}, u32[]{:S(2)}) copy-start(f32[256,256]{1,0:T(8,128)} %get-tuple-element.96) | copy-start | bytes 786436
  83.3 69.6 %collective-permute-start.32 = (f32[192,1024]{1,0:T(8,128)S(1)}, f32[192,1024]{1,0:T(8,128)}, u32[]{:S(2)}, u32[]{:S(2)}) collective-permute-start(f32[192,1024]{1,0:T(8,128)S(1)} %join.3.refs_4_), channel_id=1, source_target_pairs={{0,1},{1,0},{2,3},{3,2},{4,5},{5,4},{6,7},{7,6},{8,9},{9,8},{10,11... | collective-permute-start | bytes 2359304 | tf_op jit(solution)/shard_map/ppermute | solution.py:323
  93.0 61.2 %collective-permute-start.33 = (f32[192,1024]{1,0:T(8,128)}, f32[192,1024]{1,0:T(8,128)}, u32[]{:S(2)}, u32[]{:S(2)}) collective-permute-start(f32[192,1024]{1,0:T(8,128)} %collective-permute-done.31.refs_5_), channel_id=1, source_target_pairs={{0,1},{1,0},{2,3},{3,2},{4,5},{5,4},{6,7},{7,6},{8,9},{9,8},{10,11... | collective-permute-start | bytes 2359304 | tf_op jit(solution)/shard_map/ppermute | solution.py:323
  93.0 14.4 %collective-permute-start.17 = (f32[128,1024]{1,0:T(8,128)S(1)}, f32[128,1024]{1,0:T(8,128)}, u32[]{:S(2)}, u32[]{:S(2)}) collective-permute-start(f32[128,1024]{1,0:T(8,128)S(1)} %multiply_subtract_fusion.1), channel_id=1, source_target_pairs={{0,4},{4,0},{8,12},{12,8},{16,20},{20,16},{24,28},{28,24},{1,5},{5... | collective-permute-start | bytes 1572872 | tf_op jit(solution)/shard_map/ppermute | solution.py:326
  95.5 20.5 %collective-permute-start.25 = (f32[192,1024]{1,0:T(8,128)}, f32[192,1024]{1,0:T(8,128)}, u32[]{:S(2)}, u32[]{:S(2)}) collective-permute-start(f32[192,1024]{1,0:T(8,128)} %join.2.refs_0_), channel_id=1, source_target_pairs={{0,2},{1,3},{2,0},{3,1},{4,6},{5,7},{6,4},{7,5},{8,10},{9,11},{10,... | collective-permute-start | bytes 2359304 | tf_op jit(solution)/shard_map/ppermute | solution.py:369
  99.4 12.7 %collective-permute-start.9 = (f32[128,1024]{1,0:T(8,128)}, f32[128,1024]{1,0:T(8,128)}, u32[]{:S(2)}, u32[]{:S(2)}) collective-permute-start(f32[128,1024]{1,0:T(8,128)} %fusion.7), channel_id=1, source_target_pairs={{0,1},{1,0},{2,3},{3,2},{4,5},{5,4},{6,7},{7,6},{8,9},{9,8},{10,11... | collective-permute-start | bytes 1572872 | tf_op jit(solution)/shard_map/ppermute | solution.py:323
  107.4 2.8 %collective-permute-start.18 = (f32[128,1024]{1,0:T(8,128)}, f32[128,1024]{1,0:T(8,128)}, u32[]{:S(2)}, u32[]{:S(2)}) collective-permute-start(f32[128,1024]{1,0:T(8,128)} %collective-permute-done.17), channel_id=1, source_target_pairs={{0,1},{1,0},{2,3},{3,2},{4,5},{5,4},{6,7},{7,6},{8,9},{9,8},{10,11... | collective-permute-start | bytes 1572872 | tf_op jit(solution)/shard_map/ppermute | solution.py:323
  110.2 5.9 %collective-permute-start.6 = (f32[128,1024]{1,0:T(8,128)}, f32[128,1024]{1,0:T(8,128)S(1)}, u32[]{:S(2)}, u32[]{:S(2)}) collective-permute-start(f32[128,1024]{1,0:T(8,128)} %fusion.5), channel_id=1, source_target_pairs={{0,1},{1,0},{2,3},{3,2},{4,5},{5,4},{6,7},{7,6},{8,9},{9,8},{10,11... | collective-permute-start | bytes 1572872 | tf_op jit(solution)/shard_map/ppermute | solution.py:323
  114.1 14.2 %collective-permute-start.10 = (f32[128,1024]{1,0:T(8,128)S(1)}, f32[128,1024]{1,0:T(8,128)S(1)}, u32[]{:S(2)}, u32[]{:S(2)}) collective-permute-start(f32[128,1024]{1,0:T(8,128)S(1)} %convolution_add_fusion), channel_id=1, source_target_pairs={{0,2},{1,3},{2,0},{3,1},{4,6},{5,7},{6,4},{7,5},{8,10},{9,11},{10,... | collective-permute-start | bytes 1572872 | tf_op jit(solution)/shard_map/ppermute | solution.py:334
  116.0 13.9 %copy-start.29 = (bf16[128,1024]{1,0:T(8,128)(2,1)S(1)}, bf16[128,1024]{1,0:T(8,128)(2,1)}, u32[]{:S(2)}) copy-start(bf16[128,1024]{1,0:T(8,128)(2,1)} %copy-done.28) | copy-start | bytes 786436
  116.0 39.9 %collective-permute-start.26 = (f32[192,1024]{1,0:T(8,128)}, f32[192,1024]{1,0:T(8,128)S(1)}, u32[]{:S(2)}, u32[]{:S(2)}) collective-permute-start(f32[192,1024]{1,0:T(8,128)} %join.2.refs_0_), channel_id=1, source_target_pairs={{0,1},{1,0},{2,3},{3,2},{4,5},{5,4},{6,7},{7,6},{8,9},{9,8},{10,11... | collective-permute-start | bytes 2359304 | tf_op jit(solution)/shard_map/ppermute | solution.py:323
  116.1 39.9 %collective-permute-start.27 = (f32[192,1024]{1,0:T(8,128)}, f32[192,1024]{1,0:T(8,128)S(1)}, u32[]{:S(2)}, u32[]{:S(2)}) collective-permute-start(f32[192,1024]{1,0:T(8,128)} %collective-permute-done.25.refs_1_), channel_id=1, source_target_pairs={{0,1},{1,0},{2,3},{3,2},{4,5},{5,4},{6,7},{7,6},{8,9},{9,8},{10,11... | collective-permute-start | bytes 2359304 | tf_op jit(solution)/shard_map/ppermute | solution.py:323
  128.3 13.2 %collective-permute-start.7 = (f32[128,1024]{1,0:T(8,128)S(1)}, f32[128,1024]{1,0:T(8,128)S(1)}, u32[]{:S(2)}, u32[]{:S(2)}) collective-permute-start(f32[128,1024]{1,0:T(8,128)S(1)} %convolution_add_fusion.1), channel_id=1, source_target_pairs={{0,2},{1,3},{2,0},{3,1},{4,6},{5,7},{6,4},{7,5},{8,10},{9,11},{10,... | collective-permute-start | bytes 1572872 | tf_op jit(solution)/shard_map/ppermute | solution.py:334
  131.3 21.5 %copy-start.9 = (f32[128,1024]{1,0:T(8,128)S(1)}, f32[128,1024]{1,0:T(8,128)}, u32[]{:S(2)}) copy-start(f32[128,1024]{1,0:T(8,128)} %copy-done.7) | copy-start | bytes 1572868
  131.3 25.8 %copy-start.2 = (bf16[256,1024]{1,0:T(8,128)(2,1)S(1)}, bf16[256,1024]{1,0:T(8,128)(2,1)}, u32[]{:S(2)}) copy-start(bf16[256,1024]{1,0:T(8,128)(2,1)} %pad_maximum_fusion.2.refs_10_) | copy-start | bytes 1572868
  141.5 31.6 %collective-permute-start.21 = (f32[128,1024]{1,0:T(8,128)S(1)}, f32[128,1024]{1,0:T(8,128)S(1)}, u32[]{:S(2)}, u32[]{:S(2)}) collective-permute-start(f32[128,1024]{1,0:T(8,128)S(1)} %get-tuple-element.48), channel_id=1, source_target_pairs={{0,24},{4,28},{8,0},{12,4},{16,8},{20,12},{24,16},{28,20},{1,25},{... | collective-permute-start | bytes 1572872 | tf_op jit(solution)/shard_map/ppermute | solution.py:329
  152.9 45.1 %collective-permute-start.20 = (f32[128,1024]{1,0:T(8,128)S(1)}, f32[128,1024]{1,0:T(8,128)S(1)}, u32[]{:S(2)}, u32[]{:S(2)}) collective-permute-start(f32[128,1024]{1,0:T(8,128)S(1)} %get-tuple-element.47), channel_id=1, source_target_pairs={{0,16},{4,20},{8,24},{12,28},{16,0},{20,4},{24,8},{28,12},{1,17},{... | collective-permute-start | bytes 1572872 | tf_op jit(solution)/shard_map/ppermute | solution.py:329
  154.2 43.9 %collective-permute-start.19 = (f32[128,1024]{1,0:T(8,128)S(1)}, f32[128,1024]{1,0:T(8,128)S(1)}, u32[]{:S(2)}, u32[]{:S(2)}) collective-permute-start(f32[128,1024]{1,0:T(8,128)S(1)} %get-tuple-element.46), channel_id=1, source_target_pairs={{0,8},{4,12},{8,16},{12,20},{16,24},{20,28},{24,0},{28,4},{1,9},{5... | collective-permute-start | bytes 1572872 | tf_op jit(solution)/shard_map/ppermute | solution.py:329
  155.9 73.0 %collective-permute-start.8 = (f32[128,1024]{1,0:T(8,128)S(1)}, f32[128,1024]{1,0:T(8,128)}, u32[]{:S(2)}, u32[]{:S(2)}) collective-permute-start(f32[128,1024]{1,0:T(8,128)S(1)} %add_add_fusion.1), channel_id=1, source_target_pairs={{0,1},{1,0},{2,3},{3,2},{4,5},{5,4},{6,7},{7,6},{8,9},{9,8},{10,11... | collective-permute-start | bytes 1572872 | tf_op jit(solution)/shard_map/ppermute | solution.py:323
  155.9 42.3 %collective-permute-start.12 = (f32[2048]{0:T(1024)S(1)}, f32[2048]{0:T(1024)S(1)}, u32[]{:S(2)}, u32[]{:S(2)}) collective-permute-start(f32[2048]{0:T(1024)S(1)} %pad_maximum_fusion.9), channel_id=1, source_target_pairs={{0,1},{1,0},{2,3},{3,2},{4,5},{5,4},{6,7},{7,6},{8,9},{9,8},{10,11... | collective-permute-start | bytes 24584 | tf_op jit(solution)/shard_map/ppermute | solution.py:323
  173.1 30.6 %copy-start.25 = (f32[128,1024]{1,0:T(8,128)S(1)}, f32[128,1024]{1,0:T(8,128)}, u32[]{:S(2)}) copy-start(f32[128,1024]{1,0:T(8,128)} %copy-done.24) | copy-start | bytes 1572868
  173.1 30.6 %copy-start.50 = (f32[128]{0:T(128)S(1)}, f32[128]{0:T(128)}, u32[]{:S(2)}) copy-start(f32[128]{0:T(128)} %get-tuple-element.89) | copy-start | bytes 1540
  198.2 3.8 %collective-permute-start.13 = (f32[2816]{0:T(1024)S(1)}, f32[2816]{0:T(1024)S(1)}, u32[]{:S(2)}, u32[]{:S(2)}) collective-permute-start(f32[2816]{0:T(1024)S(1)} %pad_maximum_fusion.8), channel_id=1, source_target_pairs={{0,8},{4,12},{8,0},{12,4},{16,24},{20,28},{24,16},{28,20},{1,9},{5... | collective-permute-start | bytes 33800 | tf_op jit(solution)/shard_map/ppermute | solution.py:526
  198.3 42.6 %collective-permute-start.34 = (f32[2,128,1152]{2,1,0:T(8,128)}, f32[2,128,1152]{2,1,0:T(8,128)}, u32[]{:S(2)}, u32[]{:S(2)}) collective-permute-start(f32[2,128,1152]{2,1,0:T(8,128)} %get-tuple-element.56), channel_id=1, source_target_pairs={{0,4},{4,0},{8,12},{12,8},{16,20},{20,16},{24,28},{28,24},{1,5},{5... | collective-permute-start | bytes 3538952 | tf_op jit(solution)/shard_map/ppermute | solution.py:326
  202.0 4.6 %collective-permute-start.14 = (f32[2816]{0:T(1024)S(1)}, f32[2816]{0:T(1024)S(1)}, u32[]{:S(2)}, u32[]{:S(2)}) collective-permute-start(f32[2816]{0:T(1024)S(1)} %fusion.19), channel_id=1, source_target_pairs={{0,16},{4,20},{8,24},{12,28},{16,0},{20,4},{24,8},{28,12},{1,17},{... | collective-permute-start | bytes 33800 | tf_op jit(solution)/shard_map/ppermute | solution.py:526
  206.6 21.1 %collective-permute-start.15 = (f32[2816]{0:T(1024)S(1)}, f32[2816]{0:T(1024)S(1)}, u32[]{:S(2)}, u32[]{:S(2)}) collective-permute-start(f32[2816]{0:T(1024)S(1)} %add.247), channel_id=1, source_target_pairs={{0,4},{4,0},{8,12},{12,8},{16,20},{20,16},{24,28},{28,24},{1,5},{5... | collective-permute-start | bytes 33800 | tf_op jit(solution)/shard_map/ppermute | solution.py:326
  208.4 22.5 %collective-permute-start.11 = (f32[128,1024]{1,0:T(8,128)S(1)}, f32[128,1024]{1,0:T(8,128)}, u32[]{:S(2)}, u32[]{:S(2)}) collective-permute-start(f32[128,1024]{1,0:T(8,128)S(1)} %multiply_subtract_fusion), channel_id=1, source_target_pairs={{0,1},{1,0},{2,3},{3,2},{4,5},{5,4},{6,7},{7,6},{8,9},{9,8},{10,11... | collective-permute-start | bytes 1572872 | tf_op jit(solution)/shard_map/ppermute | solution.py:323
  210.3 28.7 %collective-permute-start.35 = (f32[1152,128]{1,0:T(8,128)}, f32[1152,128]{1,0:T(8,128)}, u32[]{:S(2)}, u32[]{:S(2)}) collective-permute-start(f32[1152,128]{1,0:T(8,128)} %get-tuple-element.58), channel_id=1, source_target_pairs={{0,4},{4,0},{8,12},{12,8},{16,20},{20,16},{24,28},{28,24},{1,5},{5... | collective-permute-start | bytes 1769480 | tf_op jit(solution)/shard_map/ppermute | solution.py:326
  (44 other events, 195.6 us)

commit v2 on v1

--- a/solution.py
+++ b/solution.py
@@ -127,6 +127,7 @@
 def gathers(dp, tensor, rows, width, hid):
     powers = tensor == 4 and dp > 2 and dp & (dp - 1) == 0
     whole = rows % (8 * tensor) == 0 and hid % (128 * tensor) == 0
+    whole = whole and (hid // tensor % 256 == 0 or hid // tensor % 384 == 0)
     return powers and whole and width % (128 * dp) == 0 and dp * rows <= 2 * width
 
 
@@ -233,13 +234,16 @@
     down_there[...] = both[:, block:]
 
 
-def far_grads(where, block, normed, cots, norm, x_near, c_near, h_near, d_gu_near, w_gu, w_down):
+def far_grads(where, block, piece, normed, cots, norm, x_near, c_near, h_near, d_gu_near, w_gu, w_down):
     rows, width = x_near.shape
     hid = w_down.shape[0]
     share = normed[0].shape[0]
     tokens = rows + 4 * share
     step = max(size for size in range(128, 513, 128) if hid % size == 0)
-    steps = hid // step
+    all_steps = hid // step
+    early = max(1, all_steps // 3)
+    start, steps = ((0, early), (early, all_steps - early))[piece]
+    hid = steps * step
     f32, bf16 = jnp.float32, jnp.bfloat16
 
     def whole(array):
@@ -261,12 +265,12 @@
                 whole(norm),
                 whole(x_near),
                 whole(c_near),
-                pl.BlockSpec((rows, step), lambda j, _: (0, j)),
-                pl.BlockSpec((rows, step), lambda j, _: (0, j)),
-                pl.BlockSpec((rows, step), lambda j, _: (0, j + steps)),
-                pl.BlockSpec((width, step), lambda j, _: (0, j)),
-                pl.BlockSpec((width, step), lambda j, _: (0, j + steps)),
-                pl.BlockSpec((step, width), lambda j, _: (j, 0)),
+                pl.BlockSpec((rows, step), lambda j, _: (0, j + start)),
+                pl.BlockSpec((rows, step), lambda j, _: (0, j + start)),
+                pl.BlockSpec((rows, step), lambda j, _: (0, j + start + all_steps)),
+                pl.BlockSpec((width, step), lambda j, _: (0, j + start)),
+                pl.BlockSpec((width, step), lambda j, _: (0, j + start + all_steps)),
+                pl.BlockSpec((step, width), lambda j, _: (j + start, 0)),
             ],
             out_specs=[
                 *[pl.BlockSpec((2, block, step), lambda j, _: (0, 0, j))] * 2,
@@ -286,7 +290,6 @@
             bytes_accessed=8 * (tokens - rows) * width + 6 * hid * width + 24 * hid * block,
             transcendentals=(tokens - rows) * hid,
         ),
-        name="far_grads",
     )(where, *normed, *cots, norm, x_near, c_near, h_near, d_gu_near, d_gu_near, w_gu, w_gu, w_down)
 
 
@@ -480,23 +483,27 @@
     grad_out = total[:, 3 * chans :].T
 
     normed2_far = gathered([after(piece, d_resid) for piece in normed2_pieces])
-    gu_here, gu_there, down_here, down_there = far_grads(
-        jnp.stack([place, along * 2 + 1 - side]),
-        block,
-        normed2_far,
-        cot_far,
-        norm_second.reshape(1, width),
-        normed2_near,
-        cot_near,
-        hidden_near,
-        d_gu_near,
-        w_gu_flat,
-        w_down,
-    )
-    gu_there = to_side(gu_there)
-    down_there = to_side(down_there)
-    grad_gu = (gu_here + gu_there).swapaxes(0, 1)
-    grad_down = down_here + down_there
+    here, there = [], []
+    for piece in range(2):
+        gu_here, gu_there, down_here, down_there = far_grads(
+            jnp.stack([place, along * 2 + 1 - side]),
+            block,
+            piece,
+            normed2_far,
+            cot_far,
+            norm_second.reshape(1, width),
+            normed2_near,
+            cot_near,
+            hidden_near,
+            d_gu_near,
+            w_gu_flat,
+            w_down,
+        )
+        here.append((gu_here, down_here))
+        there.append((to_side(gu_there), to_side(down_there)))
+    grad_gu = jnp.concatenate([a[0] + b[0] for a, b in zip(here, there)], axis=2)
+    grad_gu = grad_gu.swapaxes(0, 1)
+    grad_down = jnp.concatenate([a[1] + b[1] for a, b in zip(here, there)], axis=0)
 
     d_normed1 = d_normed1 + d_normed1_there
     xf_mine, s1_mine = mine(xf), mine(s1)

time: 245 us -> 244 us (level)
  waiting for transfers between devices: 108 us -> 101 us
  Pallas kernels: 18.4 us -> 21.9 us
  local copies, waits for them, and re-layouts: 19.2 us -> 22.3 us
    ppermute x9, waiting for transfers between devices: 24.9 us -> 18.4 us  [to_line(): lax.ppermute(values, 'dp', [(i, (i + 2 * count) % dp) for i in range(dp)])]
    ppermute x5 -> x7, waiting for transfers between devices: 30.9 us -> 26 us  [to_side(): return lax.ppermute(values, 'dp', [(i, i ^ 1) for i in range(dp)])]
    pallas_call x1 -> x2, Pallas kernels: 16.1 us -> 20.5 us  [far_grads(): pl.pallas_call(functools.partial(far_kernel, rows=rows, share=share, bloc...]
    ppermute x2, waiting for transfers between devices: 4.46 us -> 7.86 us  [body_gather(): there = lax.ppermute(small, 'dp', [(i, i ^ stride) for i in range(dp)])]
    unnamed x117 -> x129, local copies, waits for them, and re-layouts: 14.2 us -> 15.6 us
    ppermute x5 -> x7, starting transfers between devices: 6.88 us -> 7.72 us  [to_side(): return lax.ppermute(values, 'dp', [(i, i ^ 1) for i in range(dp)])]
  transfers between devices with their start and end apart: 36 -> 38, of which waited for: 12 -> 13; matrix products, arithmetic and copies ran while one was open for 21% -> 24% of each run, Pallas kernels for 8% -> 9%
where the time goes in v2:
time: 244 us
  waiting for transfers between devices  101 us (41%)
  starting transfers between devices  48.5 us (20%)
  other arithmetic  27.5 us (11%)
  local copies, waits for them, and re-layouts  22.3 us (9%)
  Pallas kernels  21.9 us (9%)
  matrix products  21 us (9%)
    ppermute x4, waiting for transfers between devices, over_chips(): lax.ppermute(values, 'tensor', [(i, i ^ stride) for i in range(tensor)])  36.7 us
    ppermute x9, starting transfers between devices, to_line(): lax.ppermute(values, 'dp', [(i, (i + 2 * count) % dp) for i in range(dp)])  28.5 us
    ppermute x7, waiting for transfers between devices, to_side(): return lax.ppermute(values, 'dp', [(i, i ^ 1) for i in range(dp)])  26 us
    pallas_call x2, Pallas kernels, far_grads(): pl.pallas_call(functools.partial(far_kernel, rows=rows, share=share, bloc...  20.5 us
    ppermute x9, waiting for transfers between devices, to_line(): lax.ppermute(values, 'dp', [(i, (i + 2 * count) % dp) for i in range(dp)])  18.4 us
    unnamed x129, local copies, waits for them, and re-layouts  15.6 us
    dot_general x7, matrix products, by_transpose(): lax.dot_general(left, right, (((1,), (1,)), ((), ())), preferred_element_...  12.4 us
    ppermute x2, waiting for transfers between devices, gathered(): there = lax.ppermute(near, 'tensor', [(i, i ^ 2) for i in range(tensor)])  9.97 us
  transfers between devices with their start and end apart: 38, of which 13 were waited for; matrix products, arithmetic and copies ran while one was open for 24% of the time, Pallas kernels for 9%

profile of v2, /device:TPU:0, one launch (start us, length us, event | category | flops | bytes accessed | tf_op | source)
XLA Modules:
  0.0 243.5 jit_solution(1656888528871678278)
XLA Ops:
  2.0 1.8 copy.23
  5.8 1.9 multiply_convert_fusion.12
  8.4 1.5 collective-permute-done
  10.2 2.9 %collective-permute-start.1 = (f32[128,1024]{1,0:T(8,128)S(1)}, f32[128,1024]{1,0:T(8,128)}, u32[]{:S(2)}, u32[]{:S(2)}) collective-permute-start(f32[128,1024]{1,0:T(8,128)S(1)} %convolution_add_fusion.3), channel_id=1, source_target_pairs={{0,2},{1,3},{2,0},{3,1},{4,6},{5,7},{6,4},{7,5},{8,10},{9,11},{10,... | collective-permute-start | bytes 1572872 | tf_op jit(solution)/shard_map/ppermute | solution.py:337
  13.3 5.7 %copy.31 = bf16[128,8,2,1152]{3,1,2,0:T(8,128)(2,1)} copy(bf16[128,8,2,1152]{3,2,1,0:T(2,128)(2,1)} %bitcast.65) | data formatting | bytes 9437184
  19.0 6.5 %collective-permute-done.1 = f32[128,1024]{1,0:T(8,128)} collective-permute-done((f32[128,1024]{1,0:T(8,128)S(1)}, f32[128,1024]{1,0:T(8,128)}, u32[]{:S(2)}, u32[]{:S(2)}) %collective-permute-start.1) | collective-permute-done | bytes 524320 | tf_op jit(solution)/shard_map/ppermute | solution.py:337
  27.0 1.8 dynamic-slice_convert_fusion
  28.8 1.8 collective-permute-start.28
  30.6 2.6 %collective-permute-start.29 = (f32[64,1024]{1,0:T(8,128)}, f32[64,1024]{1,0:T(8,128)S(1)}, u32[]{:S(2)}, u32[]{:S(2)}) collective-permute-start(f32[64,1024]{1,0:T(8,128)} %dynamic-slice_convert_fusion), channel_id=1, source_target_pairs={{0,16},{4,20},{8,24},{12,28},{16,0},{20,4},{24,8},{28,12},{1,17},{... | collective-permute-start | bytes 786440 | tf_op jit(solution)/shard_map/ppermute | solution.py:332
  33.2 1.4 collective-permute-start.30
  35.7 1.5 collective-permute-start.16
  39.8 1.4 fusion.refs_9_
  41.3 4.1 %fusion.26 = f32[256,2304]{1,0:T(8,128)S(1)} fusion(bf16[256,1024]{1,0:T(8,128)(2,1)S(1)} %fusion.refs_9_, bf16[1024,2304]{1,0:T(8,128)(2,1)} %bitcast.48), kind=kOutput, calls=%fused_computation.110 | convolution fusion | flops 1207959552 | bytes 7602176 | tf_op jit(solution)/shard_map/dot_general | solution.py:415
  45.4 2.2 multiply_convert_fusion
  47.6 2.4 fusion.3
  52.2 6.6 %collective-permute-start.24 = (f32[64,1024]{1,0:T(8,128)S(1)}, f32[64,1024]{1,0:T(8,128)S(1)}, u32[]{:S(2)}, u32[]{:S(2)}) collective-permute-start(f32[64,1024]{1,0:T(8,128)S(1)} %constant_dynamic-slice_fusion), channel_id=1, source_target_pairs={{0,24},{4,28},{8,0},{12,4},{16,8},{20,12},{24,16},{28,20},{1,25},{... | collective-permute-start | bytes 786440 | tf_op jit(solution)/shard_map/ppermute | solution.py:332
  58.9 4.3 %convolution_add_fusion.2 = f32[128,1024]{1,0:T(8,128)S(1)} fusion(f32[128,1024]{1,0:T(8,128)} %collective-permute-done.3, bf16[128,2304]{1,0:T(8,128)(2,1)S(1)} %fusion.1, bf16[1024,2304]{1,0:T(8,128)(2,1)} %bitcast.49), kind=kOutput, calls=%fused_computation.7 | convolution fusion | flops 604110848 | bytes 6356992 | tf_op jit(solution)/shard_map/dot_general | solution.py:31
  63.3 1.5 collective-permute-start.4
  66.5 1.4 multiply_reduce_fusion
  67.8 10.3 %collective-permute-done.4 = f32[128,1024]{1,0:T(8,128)S(1)} collective-permute-done((f32[128,1024]{1,0:T(8,128)S(1)}, f32[128,1024]{1,0:T(8,128)S(1)}, u32[]{:S(2)}, u32[]{:S(2)}) %collective-permute-start.4) | collective-permute-done | bytes 524320 | tf_op jit(solution)/shard_map/ppermute | solution.py:337
  79.2 1.7 multiply_convert_fusion.3.refs_4_
  80.9 1.5 fusion.27
  82.7 10.0 %collective-permute-done.31.refs_5_ = f32[192,1024]{1,0:T(8,128)} collective-permute-done((f32[192,1024]{1,0:T(8,128)S(1)}, f32[192,1024]{1,0:T(8,128)}, u32[]{:S(2)}, u32[]{:S(2)}) %collective-permute-start.31) | collective-permute-done | bytes 786464 | tf_op jit(solution)/shard_map/ppermute | solution.py:372
  92.7 1.5 collective-permute-start.17
  94.3 1.6 collective-permute-start.25
  98.3 8.9 %collective-permute-done.17 = f32[128,1024]{1,0:T(8,128)} collective-permute-done((f32[128,1024]{1,0:T(8,128)S(1)}, f32[128,1024]{1,0:T(8,128)}, u32[]{:S(2)}, u32[]{:S(2)}) %collective-permute-start.17) | collective-permute-done | bytes 524320 | tf_op jit(solution)/shard_map/ppermute | solution.py:329
  107.2 1.3 fusion.5
  112.3 1.3 add_convert_fusion.1
  113.7 1.6 convolution_add_fusion
  115.7 1.6 collective-permute-start.10
  119.5 10.4 %collective-permute-done.10 = f32[128,1024]{1,0:T(8,128)S(1)} collective-permute-done((f32[128,1024]{1,0:T(8,128)S(1)}, f32[128,1024]{1,0:T(8,128)S(1)}, u32[]{:S(2)}, u32[]{:S(2)}) %collective-permute-start.10) | collective-permute-done | bytes 524320 | tf_op jit(solution)/shard_map/ppermute | solution.py:337
  129.9 1.5 collective-permute-start.7
  131.6 1.3 conv_parts.1
  133.6 9.6 %collective-permute-done.7 = f32[128,1024]{1,0:T(8,128)S(1)} collective-permute-done((f32[128,1024]{1,0:T(8,128)S(1)}, f32[128,1024]{1,0:T(8,128)S(1)}, u32[]{:S(2)}, u32[]{:S(2)}) %collective-permute-start.7) | collective-permute-done | bytes 524320 | tf_op jit(solution)/shard_map/ppermute | solution.py:337
  143.2 11.2 %collective-permute-start.21 = (f32[128,1024]{1,0:T(8,128)S(1)}, f32[128,1024]{1,0:T(8,128)S(1)}, u32[]{:S(2)}, u32[]{:S(2)}) collective-permute-start(f32[128,1024]{1,0:T(8,128)S(1)} %get-tuple-element.52), channel_id=1, source_target_pairs={{0,24},{4,28},{8,0},{12,4},{16,8},{20,12},{24,16},{28,20},{1,25},{... | collective-permute-start | bytes 1572872 | tf_op jit(solution)/shard_map/ppermute | solution.py:332
  155.8 1.7 collective-permute-start.19
  158.7 12.7 %shard_map.161 = (f32[2,128,768]{2,1,0:T(8,128)}, f32[2,128,768]{2,1,0:T(8,128)}, f32[768,128]{1,0:T(8,128)S(1)}, f32[768,128]{1,0:T(8,128)S(1)}) custom-call(s32[2]{0:T(128)S(1)} %pad_add_fusion.where, f32[192,1024]{1,0:T(8,128)} %copy-done.3, f32[192,1024]{1,0:T(8,128)} %collective-permute-done.25.refs_1_, f32[192,1024]{1,0:T(8,128)} %copy-done.36, ...), custom_call_target="tpu_custom_call" | custom-call | flops 4831838208 | bytes 13369344 | tf_op jit(solution)/shard_map/pallas_call | solution.py:254
  171.4 7.8 %shard_map.160 = (f32[2,128,384]{2,1,0:T(8,128)S(1)}, f32[2,128,384]{2,1,0:T(8,128)S(1)}, f32[384,128]{1,0:T(8,128)S(1)}, f32[384,128]{1,0:T(8,128)S(1)}) custom-call(s32[2]{0:T(128)S(1)} %pad_add_fusion.where, f32[192,1024]{1,0:T(8,128)} %copy-done.3, f32[192,1024]{1,0:T(8,128)} %collective-permute-done.25.refs_1_, f32[192,1024]{1,0:T(8,128)} %copy-done.36, ...), custom_call_target="tpu_custom_call" | custom-call | flops 2415919104 | bytes 9830400 | tf_op jit(solution)/shard_map/pallas_call | solution.py:254
  179.2 1.6 collective-permute-start.34
  181.4 18.3 %collective-permute-done.20 = f32[128,1024]{1,0:T(8,128)S(1)} collective-permute-done((f32[128,1024]{1,0:T(8,128)S(1)}, f32[128,1024]{1,0:T(8,128)S(1)}, u32[]{:S(2)}, u32[]{:S(2)}) %collective-permute-start.20) | collective-permute-done | bytes 524320 | tf_op jit(solution)/shard_map/ppermute | solution.py:332
  199.9 3.5 %collective-permute-done.13 = f32[2816]{0:T(1024)S(1)} collective-permute-done((f32[2816]{0:T(1024)S(1)}, f32[2816]{0:T(1024)S(1)}, u32[]{:S(2)}, u32[]{:S(2)}) %collective-permute-start.13) | collective-permute-done | bytes 11296 | tf_op jit(solution)/shard_map/ppermute | solution.py:533
  203.7 4.3 %collective-permute-done.14 = f32[2816]{0:T(1024)S(1)} collective-permute-done((f32[2816]{0:T(1024)S(1)}, f32[2816]{0:T(1024)S(1)}, u32[]{:S(2)}, u32[]{:S(2)}) %collective-permute-start.14) | collective-permute-done | bytes 11296 | tf_op jit(solution)/shard_map/ppermute | solution.py:533
  208.0 1.5 collective-permute-start.15
  211.2 1.9 copy.27
  213.1 1.7 copy.28
  216.5 5.6 %collective-permute-done.36 = f32[384,128]{1,0:T(8,128)S(1)} collective-permute-done((f32[384,128]{1,0:T(8,128)S(1)}, f32[384,128]{1,0:T(8,128)S(1)}, u32[]{:S(2)}, u32[]{:S(2)}) %collective-permute-start.36) | collective-permute-done | bytes 196640 | tf_op jit(solution)/shard_map/ppermute | solution.py:329
  229.9 11.5 %collective-permute-done.35 = f32[2,128,768]{2,1,0:T(8,128)S(1)} collective-permute-done((f32[2,128,768]{2,1,0:T(8,128)}, f32[2,128,768]{2,1,0:T(8,128)S(1)}, u32[]{:S(2)}, u32[]{:S(2)}) %collective-permute-start.35) | collective-permute-done | bytes 786464 | tf_op jit(solution)/shard_map/ppermute | solution.py:329
  241.6 1.9 copy.29
  (250 shorter events, 39.2 us)
Async XLA Ops:
  3.9 93.0 %copy-start.48 = (f32[1,256]{1,0:T(1,128)}, f32[1,256]{1,0:T(1,128)S(1)}, u32[]{:S(2)}) copy-start(f32[1,256]{1,0:T(1,128)S(1)} %get-tuple-element.125) | copy-start | bytes 3076
  3.9 93.0 %copy-start.50 = (f32[1,256]{1,0:T(1,128)}, f32[1,256]{1,0:T(1,128)S(1)}, u32[]{:S(2)}) copy-start(f32[1,256]{1,0:T(1,128)S(1)} %get-tuple-element.126) | copy-start | bytes 3076
  7.9 2.1 collective-permute-start
  10.2 15.2 %collective-permute-start.1 = (f32[128,1024]{1,0:T(8,128)S(1)}, f32[128,1024]{1,0:T(8,128)}, u32[]{:S(2)}, u32[]{:S(2)}) collective-permute-start(f32[128,1024]{1,0:T(8,128)S(1)} %convolution_add_fusion.3), channel_id=1, source_target_pairs={{0,2},{1,3},{2,0},{3,1},{4,6},{5,7},{6,4},{7,5},{8,10},{9,11},{10,... | collective-permute-start | bytes 1572872 | tf_op jit(solution)/shard_map/ppermute | solution.py:337
  26.7 52.1 %copy-start.16 = (f32[128,1024]{1,0:T(8,128)}, f32[128,1024]{1,0:T(8,128)S(1)}, u32[]{:S(2)}) copy-start(f32[128,1024]{1,0:T(8,128)S(1)} %get-tuple-element.102) | copy-start | bytes 1572868
  26.9 12.9 %collective-permute-start.2 = (f32[128,1024]{1,0:T(8,128)S(1)}, f32[128,1024]{1,0:T(8,128)}, u32[]{:S(2)}, u32[]{:S(2)}) collective-permute-start(f32[128,1024]{1,0:T(8,128)S(1)} %broadcast_multiply_fusion), channel_id=1, source_target_pairs={{0,1},{1,0},{2,3},{3,2},{4,5},{5,4},{6,7},{7,6},{8,9},{9,8},{10,11... | collective-permute-start | bytes 1572872 | tf_op jit(solution)/shard_map/ppermute | solution.py:326
  28.8 21.4 %collective-permute-start.28 = (f32[64,1024]{1,0:T(8,128)}, f32[64,1024]{1,0:T(8,128)S(1)}, u32[]{:S(2)}, u32[]{:S(2)}) collective-permute-start(f32[64,1024]{1,0:T(8,128)} %dynamic-slice_convert_fusion), channel_id=1, source_target_pairs={{0,8},{4,12},{8,16},{12,20},{16,24},{20,28},{24,0},{28,4},{1,9},{5... | collective-permute-start | bytes 786440 | tf_op jit(solution)/shard_map/ppermute | solution.py:332
  30.6 20.4 %collective-permute-start.29 = (f32[64,1024]{1,0:T(8,128)}, f32[64,1024]{1,0:T(8,128)S(1)}, u32[]{:S(2)}, u32[]{:S(2)}) collective-permute-start(f32[64,1024]{1,0:T(8,128)} %dynamic-slice_convert_fusion), channel_id=1, source_target_pairs={{0,16},{4,20},{8,24},{12,28},{16,0},{20,4},{24,8},{28,12},{1,17},{... | collective-permute-start | bytes 786440 | tf_op jit(solution)/shard_map/ppermute | solution.py:332
  33.2 19.1 %collective-permute-start.30 = (f32[64,1024]{1,0:T(8,128)}, f32[64,1024]{1,0:T(8,128)S(1)}, u32[]{:S(2)}, u32[]{:S(2)}) collective-permute-start(f32[64,1024]{1,0:T(8,128)} %dynamic-slice_convert_fusion), channel_id=1, source_target_pairs={{0,24},{4,28},{8,0},{12,4},{16,8},{20,12},{24,16},{28,20},{1,25},{... | collective-permute-start | bytes 786440 | tf_op jit(solution)/shard_map/ppermute | solution.py:332
  35.7 30.2 %collective-permute-start.16 = (f32[256,1024]{1,0:T(8,128)}, f32[256,1024]{1,0:T(8,128)}, u32[]{:S(2)}, u32[]{:S(2)}) collective-permute-start(f32[256,1024]{1,0:T(8,128)} %convert_element_type.46), channel_id=1, source_target_pairs={{0,4},{4,0},{8,12},{12,8},{16,20},{20,16},{24,28},{28,24},{1,5},{5... | collective-permute-start | bytes 3145736 | tf_op jit(solution)/shard_map/ppermute | solution.py:329
  50.0 8.9 %collective-permute-start.3 = (f32[128,1024]{1,0:T(8,128)}, f32[128,1024]{1,0:T(8,128)}, u32[]{:S(2)}, u32[]{:S(2)}) collective-permute-start(f32[128,1024]{1,0:T(8,128)} %fusion.3), channel_id=1, source_target_pairs={{0,1},{1,0},{2,3},{3,2},{4,5},{5,4},{6,7},{7,6},{8,9},{9,8},{10,11... | collective-permute-start | bytes 1572872 | tf_op jit(solution)/shard_map/ppermute | solution.py:326
  50.1 32.3 %collective-permute-start.22 = (f32[64,1024]{1,0:T(8,128)S(1)}, f32[64,1024]{1,0:T(8,128)S(1)}, u32[]{:S(2)}, u32[]{:S(2)}) collective-permute-start(f32[64,1024]{1,0:T(8,128)S(1)} %constant_dynamic-slice_fusion), channel_id=1, source_target_pairs={{0,8},{4,12},{8,16},{12,20},{16,24},{20,28},{24,0},{28,4},{1,9},{5... | collective-permute-start | bytes 786440 | tf_op jit(solution)/shard_map/ppermute | solution.py:332
  51.0 41.7 %collective-permute-start.23 = (f32[64,1024]{1,0:T(8,128)S(1)}, f32[64,1024]{1,0:T(8,128)S(1)}, u32[]{:S(2)}, u32[]{:S(2)}) collective-permute-start(f32[64,1024]{1,0:T(8,128)S(1)} %constant_dynamic-slice_fusion), channel_id=1, source_target_pairs={{0,16},{4,20},{8,24},{12,28},{16,0},{20,4},{24,8},{28,12},{1,17},{... | collective-permute-start | bytes 786440 | tf_op jit(solution)/shard_map/ppermute | solution.py:332
  52.2 42.0 %collective-permute-start.24 = (f32[64,1024]{1,0:T(8,128)S(1)}, f32[64,1024]{1,0:T(8,128)S(1)}, u32[]{:S(2)}, u32[]{:S(2)}) collective-permute-start(f32[64,1024]{1,0:T(8,128)S(1)} %constant_dynamic-slice_fusion), channel_id=1, source_target_pairs={{0,24},{4,28},{8,0},{12,4},{16,8},{20,12},{24,16},{28,20},{1,25},{... | collective-permute-start | bytes 786440 | tf_op jit(solution)/shard_map/ppermute | solution.py:332
  58.9 23.6 %copy-start.2 = (f32[192,1024]{1,0:T(8,128)}, f32[192,1024]{1,0:T(8,128)S(1)}, u32[]{:S(2)}) copy-start(f32[192,1024]{1,0:T(8,128)S(1)} %join.3.refs_4_) | copy-start | bytes 2359300
  63.3 14.9 %collective-permute-start.4 = (f32[128,1024]{1,0:T(8,128)S(1)}, f32[128,1024]{1,0:T(8,128)S(1)}, u32[]{:S(2)}, u32[]{:S(2)}) collective-permute-start(f32[128,1024]{1,0:T(8,128)S(1)} %convolution_add_fusion.2), channel_id=1, source_target_pairs={{0,2},{1,3},{2,0},{3,1},{4,6},{5,7},{6,4},{7,5},{8,10},{9,11},{10,... | collective-permute-start | bytes 1572872 | tf_op jit(solution)/shard_map/ppermute | solution.py:337
  65.9 26.8 %collective-permute-start.31 = (f32[192,1024]{1,0:T(8,128)S(1)}, f32[192,1024]{1,0:T(8,128)}, u32[]{:S(2)}, u32[]{:S(2)}) collective-permute-start(f32[192,1024]{1,0:T(8,128)S(1)} %join.3.refs_4_), channel_id=1, source_target_pairs={{0,2},{1,3},{2,0},{3,1},{4,6},{5,7},{6,4},{7,5},{8,10},{9,11},{10,... | collective-permute-start | bytes 2359304 | tf_op jit(solution)/shard_map/ppermute | solution.py:372
  79.2 16.7 %collective-permute-start.5 = (f32[128,1024]{1,0:T(8,128)S(1)}, f32[128,1024]{1,0:T(8,128)S(1)}, u32[]{:S(2)}, u32[]{:S(2)}) collective-permute-start(f32[128,1024]{1,0:T(8,128)S(1)} %multiply_subtract_fusion.1), channel_id=1, source_target_pairs={{0,1},{1,0},{2,3},{3,2},{4,5},{5,4},{6,7},{7,6},{8,9},{9,8},{10,11... | collective-permute-start | bytes 1572872 | tf_op jit(solution)/shard_map/ppermute | solution.py:326
  82.5 72.0 %collective-permute-start.32 = (f32[192,1024]{1,0:T(8,128)S(1)}, f32[192,1024]{1,0:T(8,128)}, u32[]{:S(2)}, u32[]{:S(2)}) collective-permute-start(f32[192,1024]{1,0:T(8,128)S(1)} %join.3.refs_4_), channel_id=1, source_target_pairs={{0,1},{1,0},{2,3},{3,2},{4,5},{5,4},{6,7},{7,6},{8,9},{9,8},{10,11... | collective-permute-start | bytes 2359304 | tf_op jit(solution)/shard_map/ppermute | solution.py:326
  92.7 63.1 %collective-permute-start.33 = (f32[192,1024]{1,0:T(8,128)}, f32[192,1024]{1,0:T(8,128)}, u32[]{:S(2)}, u32[]{:S(2)}) collective-permute-start(f32[192,1024]{1,0:T(8,128)} %collective-permute-done.31.refs_5_), channel_id=1, source_target_pairs={{0,1},{1,0},{2,3},{3,2},{4,5},{5,4},{6,7},{7,6},{8,9},{9,8},{10,11... | collective-permute-start | bytes 2359304 | tf_op jit(solution)/shard_map/ppermute | solution.py:326
  92.7 14.4 %collective-permute-start.17 = (f32[128,1024]{1,0:T(8,128)S(1)}, f32[128,1024]{1,0:T(8,128)}, u32[]{:S(2)}, u32[]{:S(2)}) collective-permute-start(f32[128,1024]{1,0:T(8,128)S(1)} %multiply_subtract_fusion.1), channel_id=1, source_target_pairs={{0,4},{4,0},{8,12},{12,8},{16,20},{20,16},{24,28},{28,24},{1,5},{5... | collective-permute-start | bytes 1572872 | tf_op jit(solution)/shard_map/ppermute | solution.py:329
  94.3 23.3 %copy-start.3 = (f32[192,1024]{1,0:T(8,128)}, f32[192,1024]{1,0:T(8,128)S(1)}, u32[]{:S(2)}) copy-start(f32[192,1024]{1,0:T(8,128)S(1)} %join.2.refs_0_) | copy-start | bytes 2359300
  94.3 23.3 %collective-permute-start.25 = (f32[192,1024]{1,0:T(8,128)S(1)}, f32[192,1024]{1,0:T(8,128)}, u32[]{:S(2)}, u32[]{:S(2)}) collective-permute-start(f32[192,1024]{1,0:T(8,128)S(1)} %join.2.refs_0_), channel_id=1, source_target_pairs={{0,2},{1,3},{2,0},{3,1},{4,6},{5,7},{6,4},{7,5},{8,10},{9,11},{10,... | collective-permute-start | bytes 2359304 | tf_op jit(solution)/shard_map/ppermute | solution.py:372
  98.3 15.3 %collective-permute-start.9 = (f32[128,1024]{1,0:T(8,128)}, f32[128,1024]{1,0:T(8,128)}, u32[]{:S(2)}, u32[]{:S(2)}) collective-permute-start(f32[128,1024]{1,0:T(8,128)} %fusion.7), channel_id=1, source_target_pairs={{0,1},{1,0},{2,3},{3,2},{4,5},{5,4},{6,7},{7,6},{8,9},{9,8},{10,11... | collective-permute-start | bytes 1572872 | tf_op jit(solution)/shard_map/ppermute | solution.py:326
  107.1 4.6 %collective-permute-start.18 = (f32[128,1024]{1,0:T(8,128)}, f32[128,1024]{1,0:T(8,128)}, u32[]{:S(2)}, u32[]{:S(2)}) collective-permute-start(f32[128,1024]{1,0:T(8,128)} %collective-permute-done.17), channel_id=1, source_target_pairs={{0,1},{1,0},{2,3},{3,2},{4,5},{5,4},{6,7},{7,6},{8,9},{9,8},{10,11... | collective-permute-start | bytes 1572872 | tf_op jit(solution)/shard_map/ppermute | solution.py:326
  111.8 5.9 %collective-permute-start.6 = (f32[128,1024]{1,0:T(8,128)}, f32[128,1024]{1,0:T(8,128)S(1)}, u32[]{:S(2)}, u32[]{:S(2)}) collective-permute-start(f32[128,1024]{1,0:T(8,128)} %fusion.5), channel_id=1, source_target_pairs={{0,1},{1,0},{2,3},{3,2},{4,5},{5,4},{6,7},{7,6},{8,9},{9,8},{10,11... | collective-permute-start | bytes 1572872 | tf_op jit(solution)/shard_map/ppermute | solution.py:326
  115.7 14.2 %collective-permute-start.10 = (f32[128,1024]{1,0:T(8,128)S(1)}, f32[128,1024]{1,0:T(8,128)S(1)}, u32[]{:S(2)}, u32[]{:S(2)}) collective-permute-start(f32[128,1024]{1,0:T(8,128)S(1)} %convolution_add_fusion), channel_id=1, source_target_pairs={{0,2},{1,3},{2,0},{3,1},{4,6},{5,7},{6,4},{7,5},{8,10},{9,11},{10,... | collective-permute-start | bytes 1572872 | tf_op jit(solution)/shard_map/ppermute | solution.py:337
  117.6 40.0 %collective-permute-start.26 = (f32[192,1024]{1,0:T(8,128)S(1)}, f32[192,1024]{1,0:T(8,128)S(1)}, u32[]{:S(2)}, u32[]{:S(2)}) collective-permute-start(f32[192,1024]{1,0:T(8,128)S(1)} %join.2.refs_0_), channel_id=1, source_target_pairs={{0,1},{1,0},{2,3},{3,2},{4,5},{5,4},{6,7},{7,6},{8,9},{9,8},{10,11... | collective-permute-start | bytes 2359304 | tf_op jit(solution)/shard_map/ppermute | solution.py:326
  117.7 39.9 %collective-permute-start.27 = (f32[192,1024]{1,0:T(8,128)}, f32[192,1024]{1,0:T(8,128)S(1)}, u32[]{:S(2)}, u32[]{:S(2)}) collective-permute-start(f32[192,1024]{1,0:T(8,128)} %collective-permute-done.25.refs_1_), channel_id=1, source_target_pairs={{0,1},{1,0},{2,3},{3,2},{4,5},{5,4},{6,7},{7,6},{8,9},{9,8},{10,11... | collective-permute-start | bytes 2359304 | tf_op jit(solution)/shard_map/ppermute | solution.py:326
  129.9 13.3 %collective-permute-start.7 = (f32[128,1024]{1,0:T(8,128)S(1)}, f32[128,1024]{1,0:T(8,128)S(1)}, u32[]{:S(2)}, u32[]{:S(2)}) collective-permute-start(f32[128,1024]{1,0:T(8,128)S(1)} %convolution_add_fusion.1), channel_id=1, source_target_pairs={{0,2},{1,3},{2,0},{3,1},{4,6},{5,7},{6,4},{7,5},{8,10},{9,11},{10,... | collective-permute-start | bytes 1572872 | tf_op jit(solution)/shard_map/ppermute | solution.py:337
  132.9 21.5 %copy-start.17 = (f32[128,1024]{1,0:T(8,128)S(1)}, f32[128,1024]{1,0:T(8,128)}, u32[]{:S(2)}) copy-start(f32[128,1024]{1,0:T(8,128)} %copy-done.16) | copy-start | bytes 1572868
  132.9 25.8 %copy-start.5 = (bf16[256,1024]{1,0:T(8,128)(2,1)S(1)}, bf16[256,1024]{1,0:T(8,128)(2,1)}, u32[]{:S(2)}) copy-start(bf16[256,1024]{1,0:T(8,128)(2,1)} %copy-done.4) | copy-start | bytes 1572868
  132.9 25.8 %copy-start.6 = (bf16[256,1024]{1,0:T(8,128)(2,1)S(1)}, bf16[256,1024]{1,0:T(8,128)(2,1)}, u32[]{:S(2)}) copy-start(bf16[256,1024]{1,0:T(8,128)(2,1)} %pad_maximum_fusion.3.refs_10_) | copy-start | bytes 1572868
  143.2 37.7 %collective-permute-start.21 = (f32[128,1024]{1,0:T(8,128)S(1)}, f32[128,1024]{1,0:T(8,128)S(1)}, u32[]{:S(2)}, u32[]{:S(2)}) collective-permute-start(f32[128,1024]{1,0:T(8,128)S(1)} %get-tuple-element.52), channel_id=1, source_target_pairs={{0,24},{4,28},{8,0},{12,4},{16,8},{20,12},{24,16},{28,20},{1,25},{... | collective-permute-start | bytes 1572872 | tf_op jit(solution)/shard_map/ppermute | solution.py:332
  154.5 45.2 %collective-permute-start.20 = (f32[128,1024]{1,0:T(8,128)S(1)}, f32[128,1024]{1,0:T(8,128)S(1)}, u32[]{:S(2)}, u32[]{:S(2)}) collective-permute-start(f32[128,1024]{1,0:T(8,128)S(1)} %get-tuple-element.51), channel_id=1, source_target_pairs={{0,16},{4,20},{8,24},{12,28},{16,0},{20,4},{24,8},{28,12},{1,17},{... | collective-permute-start | bytes 1572872 | tf_op jit(solution)/shard_map/ppermute | solution.py:332
  155.8 43.9 %collective-permute-start.19 = (f32[128,1024]{1,0:T(8,128)S(1)}, f32[128,1024]{1,0:T(8,128)S(1)}, u32[]{:S(2)}, u32[]{:S(2)}) collective-permute-start(f32[128,1024]{1,0:T(8,128)S(1)} %get-tuple-element.50), channel_id=1, source_target_pairs={{0,8},{4,12},{8,16},{12,20},{16,24},{20,28},{24,0},{28,4},{1,9},{5... | collective-permute-start | bytes 1572872 | tf_op jit(solution)/shard_map/ppermute | solution.py:332
  157.6 68.0 %collective-permute-start.8 = (f32[128,1024]{1,0:T(8,128)S(1)}, f32[128,1024]{1,0:T(8,128)}, u32[]{:S(2)}, u32[]{:S(2)}) collective-permute-start(f32[128,1024]{1,0:T(8,128)S(1)} %add_add_fusion.1), channel_id=1, source_target_pairs={{0,1},{1,0},{2,3},{3,2},{4,5},{5,4},{6,7},{7,6},{8,9},{9,8},{10,11... | collective-permute-start | bytes 1572872 | tf_op jit(solution)/shard_map/ppermute | solution.py:326
  157.6 21.6 %collective-permute-start.12 = (f32[2048]{0:T(1024)S(1)}, f32[2048]{0:T(1024)S(1)}, u32[]{:S(2)}, u32[]{:S(2)}) collective-permute-start(f32[2048]{0:T(1024)S(1)} %pad_maximum_fusion.10), channel_id=1, source_target_pairs={{0,1},{1,0},{2,3},{3,2},{4,5},{5,4},{6,7},{7,6},{8,9},{9,8},{10,11... | collective-permute-start | bytes 24584 | tf_op jit(solution)/shard_map/ppermute | solution.py:326
  179.2 24.2 %copy-start.32 = (f32[128,1024]{1,0:T(8,128)S(1)}, f32[128,1024]{1,0:T(8,128)}, u32[]{:S(2)}) copy-start(f32[128,1024]{1,0:T(8,128)} %copy-done.31) | copy-start | bytes 1572868
  179.2 24.2 %copy-start.59 = (f32[128]{0:T(128)S(1)}, f32[128]{0:T(128)}, u32[]{:S(2)}) copy-start(f32[128]{0:T(128)} %get-tuple-element.97) | copy-start | bytes 1540
  179.2 43.4 %collective-permute-start.34 = (f32[2,128,384]{2,1,0:T(8,128)S(1)}, f32[2,128,384]{2,1,0:T(8,128)}, u32[]{:S(2)}, u32[]{:S(2)}) collective-permute-start(f32[2,128,384]{2,1,0:T(8,128)S(1)} %get-tuple-element.60), channel_id=1, source_target_pairs={{0,4},{4,0},{8,12},{12,8},{16,20},{20,16},{24,28},{28,24},{1,5},{5... | collective-permute-start | bytes 1179656 | tf_op jit(solution)/shard_map/ppermute | solution.py:329
  180.8 42.8 %collective-permute-start.37 = (f32[768,128]{1,0:T(8,128)S(1)}, f32[768,128]{1,0:T(8,128)}, u32[]{:S(2)}, u32[]{:S(2)}) collective-permute-start(f32[768,128]{1,0:T(8,128)S(1)} %get-tuple-element.66), channel_id=1, source_target_pairs={{0,4},{4,0},{8,12},{12,8},{16,20},{20,16},{24,28},{28,24},{1,5},{5... | collective-permute-start | bytes 1179656 | tf_op jit(solution)/shard_map/ppermute | solution.py:329
  199.7 3.7 %collective-permute-start.13 = (f32[2816]{0:T(1024)S(1)}, f32[2816]{0:T(1024)S(1)}, u32[]{:S(2)}, u32[]{:S(2)}) collective-permute-start(f32[2816]{0:T(1024)S(1)} %pad_maximum_fusion.9), channel_id=1, source_target_pairs={{0,8},{4,12},{8,0},{12,4},{16,24},{20,28},{24,16},{28,20},{1,9},{5... | collective-permute-start | bytes 33800 | tf_op jit(solution)/shard_map/ppermute | solution.py:533
  203.4 4.6 %collective-permute-start.14 = (f32[2816]{0:T(1024)S(1)}, f32[2816]{0:T(1024)S(1)}, u32[]{:S(2)}, u32[]{:S(2)}) collective-permute-start(f32[2816]{0:T(1024)S(1)} %fusion.19), channel_id=1, source_target_pairs={{0,16},{4,20},{8,24},{12,28},{16,0},{20,4},{24,8},{28,12},{1,17},{... | collective-permute-start | bytes 33800 | tf_op jit(solution)/shard_map/ppermute | solution.py:533
  208.0 6.8 %collective-permute-start.15 = (f32[2816]{0:T(1024)S(1)}, f32[2816]{0:T(1024)S(1)}, u32[]{:S(2)}, u32[]{:S(2)}) collective-permute-start(f32[2816]{0:T(1024)S(1)} %add.254), channel_id=1, source_target_pairs={{0,4},{4,0},{8,12},{12,8},{16,20},{20,16},{24,28},{28,24},{1,5},{5... | collective-permute-start | bytes 33800 | tf_op jit(solution)/shard_map/ppermute | solution.py:329
  210.2 17.4 %collective-permute-start.11 = (f32[128,1024]{1,0:T(8,128)S(1)}, f32[128,1024]{1,0:T(8,128)}, u32[]{:S(2)}, u32[]{:S(2)}) collective-permute-start(f32[128,1024]{1,0:T(8,128)S(1)} %multiply_subtract_fusion), channel_id=1, source_target_pairs={{0,1},{1,0},{2,3},{3,2},{4,5},{5,4},{6,7},{7,6},{8,9},{9,8},{10,11... | collective-permute-start | bytes 1572872 | tf_op jit(solution)/shard_map/ppermute | solution.py:326
  214.8 7.3 %collective-permute-start.36 = (f32[384,128]{1,0:T(8,128)S(1)}, f32[384,128]{1,0:T(8,128)S(1)}, u32[]{:S(2)}, u32[]{:S(2)}) collective-permute-start(f32[384,128]{1,0:T(8,128)S(1)} %get-tuple-element.64), channel_id=1, source_target_pairs={{0,4},{4,0},{8,12},{12,8},{16,20},{20,16},{24,28},{28,24},{1,5},{5... | collective-permute-start | bytes 589832 | tf_op jit(solution)/shard_map/ppermute | solution.py:329
  222.1 19.3 %collective-permute-start.35 = (f32[2,128,768]{2,1,0:T(8,128)}, f32[2,128,768]{2,1,0:T(8,128)S(1)}, u32[]{:S(2)}, u32[]{:S(2)}) collective-permute-start(f32[2,128,768]{2,1,0:T(8,128)} %get-tuple-element.62), channel_id=1, source_target_pairs={{0,4},{4,0},{8,12},{12,8},{16,20},{20,16},{24,28},{28,24},{1,5},{5... | collective-permute-start | bytes 2359304 | tf_op jit(solution)/shard_map/ppermute | solution.py:329
  (52 other events, 298.6 us)
